TPU v7x, 32 devices: a whole 2x2x4 slice. The times are simulated.
32 devices in a mesh: bins: 2 (over x), fsdp: 16 (over z, y, core).
Axes of the slice: x: 2, y: 2, z: 4, core: 2. Of those that a mesh axis runs over, the one named last changes fastest.
Arguments:
- tokens: bfloat16 [16384, 1152], P(('bins', 'fsdp')), may hold values from -6 to 6
- condition: float32 [2, 1152], P('bins'), may hold values from -6 to 6
- segments: int32 [16384], P('bins'), may hold values from 0 to 63, as said below
- cotangent: bfloat16 [16384, 1152], P(('bins', 'fsdp')), may hold values from -6 to 6
- target: bfloat16 [16384, 768], P(('bins', 'fsdp')), may hold values from -6 to 6
- w_ada: bfloat16 [1152, 6912], P(None, 'fsdp'), may hold values from -0.1875 to 0.1875
- w_qkv: bfloat16 [1152, 3456], P('fsdp'), may hold values from -0.1875 to 0.1875
- w_out: bfloat16 [1152, 1152], P('fsdp'), may hold values from -0.75 to 0.75
- w_fc1: bfloat16 [1152, 4608], P('fsdp'), may hold values from -0.1875 to 0.1875
- w_fc2: bfloat16 [4608, 1152], P('fsdp'), may hold values from -0.09375 to 0.09375
- w_proj1: bfloat16 [1152, 2048], P('fsdp'), may hold values from -0.1875 to 0.1875
- w_proj2: bfloat16 [2048, 2048], P('fsdp'), may hold values from -0.125 to 0.125
- w_proj3: bfloat16 [2048, 768], P('fsdp'), may hold values from -0.125 to 0.125
Outputs:
- output: bfloat16 [16384, 1152], P(('bins', 'fsdp'))
- grad_tokens: float32 [16384, 1152], P(('bins', 'fsdp'))
- grad_condition: float32 [2, 1152], P('bins')
- grad_ada: float32 [1152, 6912], P(None, 'fsdp')
- grad_qkv: float32 [1152, 3456], P('fsdp')
- grad_out: float32 [1152, 1152], P('fsdp')
- grad_fc1: float32 [1152, 4608], P('fsdp')
- grad_fc2: float32 [4608, 1152], P('fsdp')
- grad_proj1: float32 [1152, 2048], P('fsdp')
- grad_proj2: float32 [2048, 2048], P('fsdp')
- grad_proj3: float32 [2048, 768], P('fsdp')
Inputs may be any that keep to these rules, and one draw needn't show every extreme that they name: segments never fall; each aligned block of 1024 tokens holds either one image of 1024 tokens or four images of 256 tokens; images of different blocks have different ids; the first block holds one image and the last block four.
All inputs are finite; a program needn't handle non-finite values.
Results may differ from a plain program's by a relative error of at most 0.015.
Values may be sent and summed in bfloat16 or wider, within the bound.
No kernel may reach another device: no remote copies, remote signals or barrier semaphores. Data moves between devices by JAX's collectives and lax.ppermute only.
A program may use at most 320 MiB of HBM per device.

v0:
```python
from functools import partial
import jax
import jax.numpy as jnp
from jax import lax
from jax.sharding import PartitionSpec as P

HEADS = 16
HIGH = lax.Precision.HIGHEST


def swapped(block, axis, apart):
    count = lax.axis_size(axis)
    route = []
    for low in range(count):
        high = low | 1 << apart
        if high != low and high < count:
            route += [(low, high), (high, low)]
    return lax.ppermute(block, axis, route)


def bins_peer(block):
    return lax.ppermute(block, "bins", [(0, 1), (1, 0)])


def hop(block, apart):
    chips = lax.axis_size("fsdp") // 2
    route = [2 * chip for chip in range(chips // 2)]
    route = route + [chip + 1 for chip in reversed(route)]
    pairs = []
    for spot, chip in enumerate(route):
        onward = route[(spot + apart) % chips]
        pairs += [(2 * chip, 2 * onward), (2 * chip + 1, 2 * onward + 1)]
    return lax.ppermute(block, "fsdp", pairs)


def chip_at(apart):
    chips = lax.axis_size("fsdp") // 2
    chip = lax.axis_index("fsdp") // 2
    spot = jnp.where(chip % 2 == 0, chip // 2, chips - 1 - chip // 2)
    spot = (spot + apart) % chips
    return jnp.where(spot < chips // 2, 2 * spot, 2 * (chips - 1 - spot) + 1)


def doubled(block):
    count, place = (lax.axis_size("fsdp"), lax.axis_index("fsdp"))
    step = 0
    while 1 << step < count:
        other = swapped(block, "fsdp", step)
        upper = (place >> step) % 2 == 1
        block = jnp.where(upper, jnp.concatenate([other, block]), jnp.concatenate([block, other]))
        step += 1
    return block


def halved(block):
    count, place = (lax.axis_size("fsdp"), lax.axis_index("fsdp"))
    step = count.bit_length() - 1
    while step:
        step -= 1
        upper = (place >> step) % 2
        length = block.shape[0] // 2
        sent = lax.dynamic_slice_in_dim(block, (1 - upper) * length, length)
        kept = lax.dynamic_slice_in_dim(block, upper * length, length)
        block = kept + swapped(sent, "fsdp", step)
    return block


def group_sum(block):
    step = 0
    while 1 << step < lax.axis_size("fsdp"):
        block = block + swapped(block, "fsdp", step)
        step += 1
    return block


def core_rows(turned, core):
    chips = lax.axis_size("fsdp") // 2
    split = turned.reshape(chips, 2, -1, turned.shape[-1])
    picked = lax.dynamic_index_in_dim(split, core, 1, keepdims=False)
    return picked.reshape(-1, turned.shape[-1])


def chip_grad(left, right):
    core = lax.axis_index("fsdp") % 2
    turned = left.T
    mine = core_rows(turned, core)
    theirs = swapped(core_rows(turned, 1 - core), "fsdp", 0)
    rows = jnp.concatenate([mine, theirs], axis=1)
    grads = jnp.concatenate([right, swapped(right, "fsdp", 0)], axis=0)
    total = jnp.dot(rows, grads, preferred_element_type=jnp.float32)
    return total.reshape(lax.axis_size("fsdp") // 2, -1, right.shape[1])


def ring_sum(parts):
    chips, rows = parts.shape[:2]
    far = chips // 2
    cut = (rows // 2 + 7) // 8 * 8

    def part(apart):
        return lax.dynamic_index_in_dim(parts, chip_at(apart), 0, keepdims=False)

    def low(block):
        return block.astype(jnp.bfloat16)

    last = part(far)
    onward = hop(low(last[:cut]), 1)
    back = hop(low(last[cut:]), -1)
    for apart in range(far - 1, 0, -1):
        ahead, behind = (part(apart), part(-apart))
        if apart == far - 1:
            ahead = jnp.concatenate([ahead[:cut] + onward, ahead[cut:]])
            behind = jnp.concatenate([behind[:cut], behind[cut:] + back])
        else:
            ahead, behind = (ahead + onward, behind + back)
        onward, back = (hop(low(ahead), 1), hop(low(behind), -1))
    return part(0) + onward + back


def both_groups(block):
    rounded = lax.reduce_precision(block, 8, 7)
    return rounded + bins_peer(rounded.astype(jnp.bfloat16)).astype(jnp.float32)


def full_grad(left, right):
    return both_groups(ring_sum(chip_grad(left, right)))


def modulate(values, shift, scale):
    center = values - jnp.mean(values, axis=-1, keepdims=True)
    spread = jnp.mean(center * center, axis=-1, keepdims=True)
    return center * lax.rsqrt(spread + 1e-06) * (1.0 + scale) + shift


def cosine_sum(target_f, predicted):
    dots = jnp.sum(predicted * target_f, axis=-1)
    first = lax.rsqrt(jnp.sum(predicted * predicted, axis=-1) + 1e-06)
    second = lax.rsqrt(jnp.sum(target_f * target_f, axis=-1) + 1e-06)
    return jnp.sum(dots * first * second)


def product(left, right):
    return jnp.dot(left, right, preferred_element_type=jnp.float32)


def input_grad(grad, weight):
    return jnp.einsum("ne,de->nd", grad, weight, preferred_element_type=jnp.float32)


def shards(
    tokens,
    condition,
    segments,
    cotangent,
    target,
    w_ada,
    w_qkv,
    w_out,
    w_fc1,
    w_fc2,
    w_proj1,
    w_proj2,
    w_proj3,
):
    count = tokens.shape[0]
    width = tokens.shape[1]
    head_size = width // HEADS
    factor = head_size ** (-0.5)
    tokens_f = tokens.astype(jnp.float32)
    target_f = target.astype(jnp.float32)
    silu_cond, silu_back = jax.vjp(jax.nn.silu, condition)
    cond_low = silu_cond.astype(jnp.bfloat16)
    mod_cols = product(cond_low, w_ada)
    modulation = doubled(mod_cols.reshape(-1)).reshape(6, width)
    block_set = (
        lax.all_gather(w_qkv, "fsdp", axis=0, tiled=True),
        lax.all_gather(w_out, "fsdp", axis=0, tiled=True),
        lax.all_gather(w_fc1, "fsdp", axis=0, tiled=True),
        lax.all_gather(w_fc2, "fsdp", axis=0, tiled=True),
    )
    head_set = (
        lax.all_gather(w_proj1, "fsdp", axis=0, tiled=True),
        lax.all_gather(w_proj2, "fsdp", axis=0, tiled=True),
        lax.all_gather(w_proj3, "fsdp", axis=0, tiled=True),
    )
    full_qkv, full_out, full_fc1, full_fc2 = block_set
    head_first, head_second, head_third = head_set
    h_one, norm_one_back = jax.vjp(modulate, tokens_f, modulation[0], modulation[1])
    in_one = h_one.astype(jnp.bfloat16)
    qkv_low = product(in_one, full_qkv).astype(jnp.bfloat16).reshape(count, 3, HEADS, head_size)
    queries = qkv_low[:, 0]
    pair_own = jnp.stack([qkv_low[:, 1], qkv_low[:, 2]])
    pair_peer = swapped(pair_own, "fsdp", 0)
    keys_all = jnp.concatenate([pair_own[0], pair_peer[0]], axis=0)
    values_all = jnp.concatenate([pair_own[1], pair_peer[1]], axis=0)
    place = lax.axis_index("fsdp")
    own_ids = lax.dynamic_slice_in_dim(segments, place * count, count)
    peer_ids = lax.dynamic_slice_in_dim(segments, jnp.bitwise_xor(place, 1) * count, count)
    same = own_ids[:, None] == jnp.concatenate([own_ids, peer_ids])[None, :]
    raw = jnp.einsum("qhd,khd->hqk", queries, keys_all, preferred_element_type=jnp.float32) * factor
    masked = jnp.where(same[None], raw, -1e30)
    highest = jnp.max(masked, axis=-1, keepdims=True)
    expo = jnp.exp(masked - highest)
    totals = jnp.sum(expo, axis=-1, keepdims=True)
    log_total = highest + jnp.log(totals)
    probs_low = (expo / totals).astype(jnp.bfloat16)
    attended = jnp.einsum("hqk,khd->qhd", probs_low, values_all, preferred_element_type=jnp.float32)
    attended = attended.astype(jnp.bfloat16).reshape(count, width)
    branch_one = product(attended, full_out)
    resid_one = tokens_f + modulation[2] * branch_one
    h_two, norm_two_back = jax.vjp(modulate, resid_one, modulation[3], modulation[4])
    in_two = h_two.astype(jnp.bfloat16)
    hidden_pre = product(in_two, full_fc1)
    hidden_act, gelu_back = jax.vjp(partial(jax.nn.gelu, approximate=True), hidden_pre)
    hidden_low = hidden_act.astype(jnp.bfloat16)
    branch_two = product(hidden_low, full_fc2)
    result = resid_one + modulation[5] * branch_two
    result_low = result.astype(jnp.bfloat16)
    first_act, first_back = jax.vjp(jax.nn.silu, product(result_low, head_first))
    first_low = first_act.astype(jnp.bfloat16)
    second_act, second_back = jax.vjp(jax.nn.silu, product(first_low, head_second))
    second_low = second_act.astype(jnp.bfloat16)
    predicted = product(second_low, head_third)
    cos_total, cos_back = jax.vjp(partial(cosine_sum, target_f), predicted)
    (grad_pred,) = cos_back(jnp.float32(-1.0))
    grad_pred_low = grad_pred.astype(jnp.bfloat16)
    grad_third = full_grad(second_low, grad_pred_low)
    (grad_second_pre,) = second_back(input_grad(grad_pred_low, head_third))
    grad_second_low = grad_second_pre.astype(jnp.bfloat16)
    grad_second = full_grad(first_low, grad_second_low)
    (grad_first_pre,) = first_back(input_grad(grad_second_low, head_second))
    grad_first_low = grad_first_pre.astype(jnp.bfloat16)
    grad_first = full_grad(result_low, grad_first_low)
    d_result = cotangent.astype(jnp.float32) + input_grad(grad_first_low, head_first)
    grad_gate_two = jnp.sum(d_result * branch_two, axis=0)
    d_branch_two = (d_result * modulation[5]).astype(jnp.bfloat16)
    grad_fc2 = full_grad(hidden_low, d_branch_two)
    (d_pre,) = gelu_back(input_grad(d_branch_two, full_fc2))
    d_pre_low = d_pre.astype(jnp.bfloat16)
    grad_fc1 = full_grad(in_two, d_pre_low)
    d_resid_part, grad_shift_two, grad_scale_two = norm_two_back(input_grad(d_pre_low, full_fc1))
    d_resid = d_result + d_resid_part
    grad_gate_one = jnp.sum(d_resid * branch_one, axis=0)
    d_branch_one = (d_resid * modulation[2]).astype(jnp.bfloat16)
    grad_out = full_grad(attended, d_branch_one)
    d_attended = (
        input_grad(d_branch_one, full_out).astype(jnp.bfloat16).reshape(count, HEADS, head_size)
    )
    again_raw = (
        jnp.einsum("qhd,khd->hqk", queries, keys_all, preferred_element_type=jnp.float32) * factor
    )
    probs = jnp.exp(jnp.where(same[None], again_raw, -1e30) - log_total)
    probs_again = probs.astype(jnp.bfloat16)
    d_probs = jnp.einsum("qhd,khd->hqk", d_attended, values_all, preferred_element_type=jnp.float32)
    centre = jnp.sum(d_probs * probs, axis=-1, keepdims=True)
    d_scores = (probs * (d_probs - centre)).astype(jnp.bfloat16)
    d_queries = (
        jnp.einsum("hqk,khd->qhd", d_scores, keys_all, preferred_element_type=jnp.float32) * factor
    )
    d_keys = (
        jnp.einsum("hqk,qhd->khd", d_scores, queries, preferred_element_type=jnp.float32) * factor
    )
    d_values = jnp.einsum(
        "hqk,qhd->khd", probs_again, d_attended, preferred_element_type=jnp.float32
    )
    from_peer = swapped(jnp.stack([d_keys[count:], d_values[count:]]), "fsdp", 0)
    keys_grad = d_keys[:count] + from_peer[0]
    values_grad = d_values[:count] + from_peer[1]
    d_qkv = (
        jnp.stack([d_queries, keys_grad, values_grad], axis=1)
        .reshape(count, 3 * width)
        .astype(jnp.bfloat16)
    )
    grad_qkv = full_grad(in_one, d_qkv)
    d_tok_part, grad_shift_one, grad_scale_one = norm_one_back(input_grad(d_qkv, full_qkv))
    grad_tokens = d_resid + d_tok_part
    d_modulation = jnp.stack(
        [
            grad_shift_one,
            grad_scale_one,
            grad_gate_one,
            grad_shift_two,
            grad_scale_two,
            grad_gate_two,
        ]
    ).reshape(6 * width)
    mod_grad_cols = halved(d_modulation).reshape(1, -1)
    cond_part = jnp.dot(mod_grad_cols, w_ada.astype(jnp.float32).T, precision=HIGH)
    (grad_condition,) = silu_back(group_sum(cond_part))
    group = lax.axis_index("bins")
    cond_low_f = cond_low.astype(jnp.float32)
    other_cond, other_cols = (bins_peer(cond_low_f), bins_peer(mod_grad_cols))
    first_cond = jnp.where(group == 0, cond_low_f, other_cond)
    last_cond = jnp.where(group == 0, other_cond, cond_low_f)
    first_cols = jnp.where(group == 0, mod_grad_cols, other_cols)
    last_cols = jnp.where(group == 0, other_cols, mod_grad_cols)
    grad_ada = first_cond.T * first_cols + last_cond.T * last_cols
    return (
        result_low,
        grad_tokens,
        grad_condition,
        grad_ada,
        grad_qkv,
        grad_out,
        grad_fc1,
        grad_fc2,
        grad_first,
        grad_second,
        grad_third,
    )


def solution(mesh):
    placed = (
        P(("bins", "fsdp"), None),
        P("bins", None),
        P("bins"),
        P(("bins", "fsdp"), None),
        P(("bins", "fsdp"), None),
        P(None, "fsdp"),
        P("fsdp", None),
        P("fsdp", None),
        P("fsdp", None),
        P("fsdp", None),
        P("fsdp", None),
        P("fsdp", None),
        P("fsdp", None),
    )
    return jax.shard_map(
        shards,
        mesh=mesh,
        in_specs=placed,
        out_specs=(
            P(("bins", "fsdp"), None),
            P(("bins", "fsdp"), None),
            P("bins", None),
            P(None, "fsdp"),
            P("fsdp", None),
            P("fsdp", None),
            P("fsdp", None),
            P("fsdp", None),
            P("fsdp", None),
            P("fsdp", None),
            P("fsdp", None),
        ),
        check_vma=False,
    )
```

profile of v0, /device:TPU:0, one launch (start us, length us, event | category | flops | bytes accessed | tf_op | source)
XLA Modules:
  0.0 1121.1 jit_solution(2670835607985499530)
XLA Ops:
  27.0 58.8 %all-gather.8.cloned.1.call-done = bf16[1152,3456]{1,0:T(8,128)(2,1)} async-done(((bf16[72,3456]{1,0:T(8,128)(2,1)}), bf16[1152,3456]{1,0:T(8,128)(2,1)}) %all-gather.8.cloned.1.call-update) | async-done | bytes 7962640 | tf_op jit(solution)/shard_map/all_gather | solution.py:175
  85.8 9.9 convolution_convert_fusion
  95.7 5.8 copy.29
  114.2 16.7 %fusion.244 = (f32[16,512]{1,0:T(8,128)S(1)}, f32[16,512,1024]{2,1,0:T(8,128)}) fusion(bf16[512,16,72]{0,2,1:T(8,128)(2,1)S(1)} %get-tuple-element.67, bf16[512,16,72]{0,2,1:T(8,128)(2,1)S(1)} %get-tuple-element.54, bf16[512,3,16,72]{0,3,2,1:T(8,128)(2,1)} %bitcast.488, pred[512,1024]{1,0:T(8,128)(4,1)S(1)} %copy-done.46), kind=kOutput, calls=%fused_computation.452 | convolution fusion | flops 1237835776 | bytes 37650432 | tf_op jit(solution)/shard_map/qhd,khd->hqk/dot_general | solution.py:199
  130.8 14.6 %fusion = f32[16,512]{1,0:T(8,128)S(1)} fusion(f32[16,512,1024]{2,1,0:T(8,128)} %get-tuple-element.101, f32[16,512]{1,0:T(8,128)S(1)} %get-tuple-element.100), kind=kLoop, calls=%fused_computation.6 | loop fusion | flops 16769024 | bytes 33619968 | tf_op jit(solution)/shard_map/reduce_sum | solution.py:203
  146.1 14.9 %fusion.98 = bf16[16,72,512]{2,1,0:T(8,128)(2,1)S(1)} fusion(f32[16,512,1024]{2,1,0:T(8,128)} %get-tuple-element.101, f32[16,512]{1,0:T(8,128)S(1)} %fusion, f32[16,512]{1,0:T(8,128)S(1)} %get-tuple-element.100, bf16[512,16,72]{0,2,1:T(8,128)(2,1)} %get-tuple-element.66, bf16[512,16,72]{0,2,1:T(8,128)(2,1)} %get-tuple-element.52), kind=kOutput, calls=%fused_computation.150 | convolution fusion | flops 1238433792 | bytes 37158912 | tf_op jit(solution)/shard_map/hqk,khd->qhd/dot_general | solution.py:206
  168.2 51.1 %all-gather.12.cloned.1.call-done = bf16[1152,4608]{1,0:T(8,128)(2,1)} async-done(((bf16[72,4608]{1,0:T(8,128)(2,1)}), bf16[1152,4608]{1,0:T(8,128)(2,1)}) %all-gather.12.cloned.1.call-update) | async-done | bytes 10616848 | tf_op jit(solution)/shard_map/all_gather | solution.py:177
  219.3 15.4 %fusion.20 = (bf16[4608,512]{0,1:T(8,128)(2,1)}, f32[512,4608]{1,0:T(8,128)}) fusion(bf16[1152,4608]{1,0:T(8,128)(2,1)} %all-gather.12.cloned.1.call-done, f32[512,1152]{1,0:T(8,128)} %copy-done.5, f32[1152]{0:T(1024)S(1)} %get-tuple-element.91, f32[1152]{0:T(1024)S(1)} %get-tuple-element.92, f32[512]{0:T(512)S(1)} %fusion.216, ...), kind=kOutput, calls=%fused_computation.28 | convolution fusion | flops 5460000768 | bytes 27145216 | tf_op jit(solution)/shard_map/dot_general | solution.py:142
  234.8 73.6 %all-gather.14.cloned.1.call-done = bf16[4608,1152]{1,0:T(8,128)(2,1)} async-done(((bf16[288,1152]{1,0:T(8,128)(2,1)}), bf16[4608,1152]{1,0:T(8,128)(2,1)}) %all-gather.14.cloned.1.call-update) | async-done | bytes 10616848 | tf_op jit(solution)/shard_map/all_gather | solution.py:178
  308.4 14.1 %add_convert_fusion = (bf16[512,1152]{1,0:T(8,128)(2,1)}, f32[512,1152]{1,0:T(8,128)}) fusion(f32[512,1152]{1,0:T(8,128)S(1)} %copy-done.6, f32[1152]{0:T(1024)S(1)} %get-tuple-element.90, bf16[4608,1152]{1,0:T(8,128)(2,1)} %all-gather.14.cloned.1.call-done, f32[512,4608]{1,0:T(8,128)} %get-tuple-element.114), kind=kOutput, calls=%fused_computation.127 | convolution fusion | flops 5458821120 | bytes 25956864 | tf_op jit(solution)/shard_map/dot_general | solution.py:142
  322.4 39.6 %all-gather.16.cloned.1.call-done = bf16[1152,2048]{1,0:T(8,128)(2,1)} async-done(((bf16[72,2048]{1,0:T(8,128)(2,1)}), bf16[1152,2048]{1,0:T(8,128)(2,1)}) %all-gather.16.cloned.1.call-update) | async-done | bytes 4718608 | tf_op jit(solution)/shard_map/all_gather | solution.py:181
  362.1 8.6 fusion.54
  370.7 66.9 %all-gather.18.cloned.1.call-done = bf16[2048,2048]{1,0:T(8,128)(2,1)} async-done(((bf16[128,2048]{1,0:T(8,128)(2,1)}), bf16[2048,2048]{1,0:T(8,128)(2,1)}) %all-gather.18.cloned.1.call-update) | async-done | bytes 8388624 | tf_op jit(solution)/shard_map/all_gather | solution.py:182
  437.6 12.3 %fusion.55 = (bf16[2048,512]{0,1:T(8,128)(2,1)}, f32[512,2048]{1,0:T(8,128)}) fusion(bf16[2048,2048]{1,0:T(8,128)(2,1)} %all-gather.18.cloned.1.call-done, f32[512,2048]{1,0:T(8,128)} %get-tuple-element.116), kind=kOutput, calls=%fused_computation.77 | convolution fusion | flops 4305453056 | bytes 18874368 | tf_op jit(solution)/shard_map/dot_general | solution.py:142
  449.9 33.4 %all-gather.20.cloned.1.call-done = bf16[2048,768]{1,0:T(8,128)(2,1)} async-done(((bf16[128,768]{1,0:T(8,128)(2,1)}), bf16[2048,768]{1,0:T(8,128)(2,1)}) %all-gather.20.cloned.1.call-update) | async-done | bytes 3145744 | tf_op jit(solution)/shard_map/all_gather | solution.py:183
  483.3 6.0 fusion.91
  491.5 5.3 fusion.36
  496.8 8.9 fusion.39
  511.7 16.3 %fusion.12 = bf16[512,4608]{1,0:T(8,128)(2,1)} fusion(f32[512,4608]{1,0:T(8,128)} %get-tuple-element.114, bf16[512,1152]{1,0:T(8,128)(2,1)S(1)} %get-tuple-element.106, bf16[4608,1152]{1,0:T(8,128)(2,1)} %all-gather.14.cloned.1.call-done), kind=kOutput, calls=%fused_computation.20 | convolution fusion | flops 5483003904 | bytes 25952256 | tf_op jit(solution)/shard_map/ne,de->nd/dot_general | solution.py:146
  527.9 11.8 %multiply_reduce_fusion.2 = (f32[1152]{0:T(1024)S(1)}, f32[512]{0:T(512)S(1)}, f32[1152]{0:T(1024)S(1)}, f32[512,1152]{1,0:T(8,128)S(1)}) fusion(f32[512,1152]{1,0:T(8,128)S(1)} %copy-done.6, f32[512]{0:T(512)S(1)} %fusion.216, f32[512]{0:T(512)S(1)} %broadcast_multiply_fusion, f32[1152]{0:T(1024)S(1)} %get-tuple-element.92, ...), kind=kOutput, calls=%fused_computation.119 | convolution fusion | flops 5440534016 | bytes 20073984 | tf_op jit(solution)/shard_map/ne,de->nd/dot_general | solution.py:146
  550.0 15.6 %fusion.78 = f32[1024,16,72]{0,2,1:T(8,128)} fusion(bf16[512,16,72]{0,2,1:T(8,128)(2,1)S(1)} %bitcast.490, f32[16,512,1024]{2,1,0:T(8,128)} %get-tuple-element.101, f32[16,512]{1,0:T(8,128)S(1)} %copy-done.36), kind=kOutput, calls=%fused_computation.130 | convolution fusion | flops 1224736768 | bytes 39485440 | tf_op jit(solution)/shard_map/hqk,qhd->khd/dot_general | solution.py:262
  565.6 22.3 %multiply_reduce_fusion = (f32[16,512]{1,0:T(8,128)S(1)}, f32[16,512,1024]{2,1,0:T(8,128)}) fusion(f32[16,512,1024]{2,1,0:T(8,128)} %get-tuple-element.101, f32[16,512]{1,0:T(8,128)S(1)} %copy-done.36, bf16[512,16,72]{0,2,1:T(8,128)(2,1)S(1)} %bitcast.491, bf16[512,16,72]{0,2,1:T(8,128)(2,1)S(1)} %copy-done.24, bf16[512,16,72]{0,2,1:T(8,128)(2,1)S(1)} %copy-done.23), kind=kOutput, calls=%fused_computation.1 | convolution fusion | flops 1237835776 | bytes 70713344 | tf_op jit(solution)/shard_map/qhd,khd->hqk/dot_general | solution.py:253
  588.6 27.8 %multiply_convert_fusion = bf16[16,512,1024]{2,1,0:T(8,128)(2,1)} fusion(f32[16,512,1024]{2,1,0:T(8,128)} %get-tuple-element.110, f32[16,512,1024]{2,1,0:T(8,128)} %get-tuple-element.101, f32[16,512]{1,0:T(8,128)S(1)} %get-tuple-element.109, f32[16,512]{1,0:T(8,128)S(1)} %copy-done.36), kind=kLoop, calls=%fused_computation | loop fusion | flops 33554432 | bytes 83951616 | tf_op jit(solution)/shard_map/convert_element_type | solution.py:255
  616.5 11.4 %multiply_bitcast_fusion = f32[1024,16,72]{0,2,1:T(8,128)} fusion(bf16[16,512,1024]{2,1,0:T(8,128)(2,1)} %multiply_convert_fusion, bf16[512,3,16,72]{0,3,2,1:T(8,128)(2,1)} %bitcast.489), kind=kOutput, calls=%fused_computation.46 | convolution fusion | flops 1209139200 | bytes 22675456 | tf_op jit(solution)/shard_map/hqk,qhd->khd/dot_general | solution.py:260
  630.7 7.0 copy.33
  650.3 11.8 %constant_dynamic-slice_fusion.1 = (bf16[8,1,128,512]{2,1,0,3:T(2,128)(2,1)}, bf16[8,1,128,512]{2,1,0,3:T(2,128)(2,1)}, bf16[8,1,128,512]{2,1,0,3:T(2,128)(2,1)}, bf16[8,1,128,512]{2,1,0,3:T(2,128)(2,1)}) fusion(bf16[8,2,128,512]{2,1,0,3:T(2,128)(2,1)S(1)} %reshape.384, s32[]{:T(128)S(6)} %select_n.809, s32[]{:T(128)S(6)} %select_n.810, ...), kind=kLoop, calls=%fused_computation.374 | loop fusion | bytes 8388616 | tf_op jit(solution)/shard_map/jit(dynamic_index_in_dim)/dynamic_slice | solution.py:79
  662.1 5.8 copy.42
  680.8 6.0 copy.39
  691.0 10.4 fusion.100
  775.0 6.4 fusion.44
  803.6 8.8 fusion.29
  815.0 6.6 collective-permute-done.63
  834.5 9.1 collective-permute-done.64
  853.9 6.2 collective-permute-done.75
  861.6 9.7 collective-permute-done.52
  886.6 9.3 collective-permute-done.56
  913.0 8.1 collective-permute-done.57
  930.2 8.9 fusion.66
  943.9 8.5 fusion.21
  981.8 5.7 collective-permute-done.44
  989.2 8.6 collective-permute-done.40
  1005.2 9.5 collective-permute-done.41
  1023.7 7.2 fusion.25
  1040.7 9.2 collective-permute-done.19
  1054.2 10.1 collective-permute-done.20
  1071.7 8.4 collective-permute-done.24
  1082.3 10.8 collective-permute-done.47
  1100.5 6.7 collective-permute-done.48
  (536 shorter events, 344.7 us)
Async XLA Ops:
  7.2 78.6 %all-gather.8.cloned.1.call-start = ((), (), s32[]{:S(2)}) async-start(), calls=%async_computation | async-start | bytes 8460288 | tf_op jit(solution)/shard_map/all_gather | solution.py:175
  8.0 153.1 %all-gather.10.cloned.1.call-start = ((), (), s32[]{:S(2)}) async-start(), calls=%async_computation.1 | async-start | bytes 2820096 | tf_op jit(solution)/shard_map/all_gather | solution.py:176
  8.7 210.6 %all-gather.12.cloned.1.call-start = ((), (), s32[]{:S(2)}) async-start(), calls=%async_computation.2 | async-start | bytes 11280384 | tf_op jit(solution)/shard_map/all_gather | solution.py:177
  9.4 298.9 %all-gather.14.cloned.1.call-start = ((), (), s32[]{:S(2)}) async-start(), calls=%async_computation.3 | async-start | bytes 11280384 | tf_op jit(solution)/shard_map/all_gather | solution.py:178
  10.0 352.1 %all-gather.16.cloned.1.call-start = ((), (), s32[]{:S(2)}) async-start(), calls=%async_computation.4 | async-start | bytes 5013504 | tf_op jit(solution)/shard_map/all_gather | solution.py:181
  10.6 427.0 %all-gather.18.cloned.1.call-start = ((), (), s32[]{:S(2)}) async-start(), calls=%async_computation.5 | async-start | bytes 8912896 | tf_op jit(solution)/shard_map/all_gather | solution.py:182
  11.2 472.2 %all-gather.20.cloned.1.call-start = ((), (), s32[]{:S(2)}) async-start(), calls=%async_computation.6 | async-start | bytes 3342336 | tf_op jit(solution)/shard_map/all_gather | solution.py:183
  168.0 543.8 %collective-permute-start.27 = (bf16[576,512]{1,0:T(8,128)(2,1)}, bf16[576,512]{1,0:T(8,128)(2,1)}, u32[]{:S(2)}, u32[]{:S(2)}) collective-permute-start(bf16[576,512]{1,0:T(8,128)(2,1)} %bitcast.49), channel_id=1, source_target_pairs={{0,1},{1,0},{2,3},{3,2},{4,5},{5,4},{6,7},{7,6},{8,9},{9,8},{10,11... | collective-permute-start | bytes 1769480 | tf_op jit(solution)/shard_map/ppermute | solution.py:18
  587.9 124.9 %collective-permute-start.28 = (bf16[512,1152]{1,0:T(8,128)(2,1)}, bf16[512,1152]{1,0:T(8,128)(2,1)}, u32[]{:S(2)}, u32[]{:S(2)}) collective-permute-start(bf16[512,1152]{1,0:T(8,128)(2,1)} %multiply_convert_fusion.6), channel_id=1, source_target_pairs={{0,1},{1,0},{2,3},{3,2},{4,5},{5,4},{6,7},{7,6},{8,9},{9,8},{10,11... | collective-permute-start | bytes 3538952 | tf_op jit(solution)/shard_map/ppermute | solution.py:18
  588.1 176.5 %collective-permute-start.61 = (bf16[512,2048]{1,0:T(8,128)(2,1)}, bf16[512,2048]{1,0:T(8,128)(2,1)}, u32[]{:S(2)}, u32[]{:S(2)}) collective-permute-start(bf16[512,2048]{1,0:T(8,128)(2,1)} %fusion.39), channel_id=1, source_target_pairs={{0,1},{1,0},{2,3},{3,2},{4,5},{5,4},{6,7},{7,6},{8,9},{9,8},{10,11... | collective-permute-start | bytes 6291464 | tf_op jit(solution)/shard_map/ppermute | solution.py:18
  588.4 113.0 %collective-permute-start.83 = (bf16[512,768]{1,0:T(8,128)(2,1)}, bf16[512,768]{1,0:T(8,128)(2,1)}, u32[]{:S(2)}, u32[]{:S(2)}) collective-permute-start(bf16[512,768]{1,0:T(8,128)(2,1)} %fusion.94), channel_id=1, source_target_pairs={{0,1},{1,0},{2,3},{3,2},{4,5},{5,4},{6,7},{7,6},{8,9},{9,8},{10,11... | collective-permute-start | bytes 2359304 | tf_op jit(solution)/shard_map/ppermute | solution.py:18
  667.9 33.5 %collective-permute-start.82 = (bf16[1024,512]{1,0:T(8,128)(2,1)}, bf16[1024,512]{1,0:T(8,128)(2,1)}, u32[]{:S(2)}, u32[]{:S(2)}) collective-permute-start(bf16[1024,512]{1,0:T(8,128)(2,1)} %bitcast.127), channel_id=1, source_target_pairs={{0,1},{1,0},{2,3},{3,2},{4,5},{5,4},{6,7},{7,6},{8,9},{9,8},{10,11... | collective-permute-start | bytes 3145736 | tf_op jit(solution)/shard_map/ppermute | solution.py:18
  710.2 63.3 %collective-permute-start.72 = (bf16[512,2048]{1,0:T(8,128)(2,1)S(1)}, bf16[512,2048]{1,0:T(8,128)(2,1)S(1)}, u32[]{:S(2)}, u32[]{:S(2)}) collective-permute-start(bf16[512,2048]{1,0:T(8,128)(2,1)S(1)} %copy-done.74), channel_id=1, source_target_pairs={{0,1},{1,0},{2,3},{3,2},{4,5},{5,4},{6,7},{7,6},{8,9},{9,8},{10,11... | collective-permute-start | bytes 6291464 | tf_op jit(solution)/shard_map/ppermute | solution.py:18
  711.8 52.2 %collective-permute-start.60 = (bf16[576,512]{1,0:T(8,128)(2,1)S(1)}, bf16[576,512]{1,0:T(8,128)(2,1)S(1)}, u32[]{:S(2)}, u32[]{:S(2)}) collective-permute-start(bf16[576,512]{1,0:T(8,128)(2,1)S(1)} %bitcast.573), channel_id=1, source_target_pairs={{0,1},{1,0},{2,3},{3,2},{4,5},{5,4},{6,7},{7,6},{8,9},{9,8},{10,11... | collective-permute-start | bytes 1769480 | tf_op jit(solution)/shard_map/ppermute | solution.py:18
  711.9 14.8 %collective-permute-start.85 = (bf16[128,768]{1,0:T(8,128)(2,1)S(1)}, bf16[128,768]{1,0:T(8,128)(2,1)S(1)}, u32[]{:S(2)}, u32[]{:S(2)}) collective-permute-start(bf16[128,768]{1,0:T(8,128)(2,1)S(1)} %pad_maximum_fusion.21), channel_id=1, source_target_pairs={{0,4},{1,5},{4,8},{5,9},{8,12},{9,13},{12,14},{13,15},{14,10},{15,... | collective-permute-start | bytes 589832 | tf_op jit(solution)/shard_map/ppermute | solution.py:33
  759.9 184.0 %collective-permute-start.39 = (bf16[512,4608]{1,0:T(8,128)(2,1)}, bf16[512,4608]{1,0:T(8,128)(2,1)}, u32[]{:S(2)}, u32[]{:S(2)}) collective-permute-start(bf16[512,4608]{1,0:T(8,128)(2,1)} %fusion.12), channel_id=1, source_target_pairs={{0,1},{1,0},{2,3},{3,2},{4,5},{5,4},{6,7},{7,6},{8,9},{9,8},{10,11... | collective-permute-start | bytes 14155784 | tf_op jit(solution)/shard_map/ppermute | solution.py:18
  763.9 37.0 %collective-permute-start.50 = (bf16[512,1152]{1,0:T(8,128)(2,1)S(1)}, bf16[512,1152]{1,0:T(8,128)(2,1)}, u32[]{:S(2)}, u32[]{:S(2)}) collective-permute-start(bf16[512,1152]{1,0:T(8,128)(2,1)S(1)} %copy-done.77), channel_id=1, source_target_pairs={{0,1},{1,0},{2,3},{3,2},{4,5},{5,4},{6,7},{7,6},{8,9},{9,8},{10,11... | collective-permute-start | bytes 3538952 | tf_op jit(solution)/shard_map/ppermute | solution.py:18
  764.0 160.5 %collective-permute-start.5 = (f32[2,512,16,72]{1,3,2,0:T(8,128)}, f32[2,512,16,72]{1,3,2,0:T(8,128)}, u32[]{:S(2)}, u32[]{:S(2)}) collective-permute-start(f32[2,512,16,72]{1,3,2,0:T(8,128)} %pad_maximum_fusion), channel_id=1, source_target_pairs={{0,1},{1,0},{2,3},{3,2},{4,5},{5,4},{6,7},{7,6},{8,9},{9,8},{10,11... | collective-permute-start | bytes 14155784 | tf_op jit(solution)/shard_map/ppermute | solution.py:18
  773.4 28.9 %collective-permute-start.49 = (bf16[2304,512]{1,0:T(8,128)(2,1)S(1)}, bf16[2304,512]{1,0:T(8,128)(2,1)S(1)}, u32[]{:S(2)}, u32[]{:S(2)}) collective-permute-start(bf16[2304,512]{1,0:T(8,128)(2,1)S(1)} %bitcast.565), channel_id=1, source_target_pairs={{0,1},{1,0},{2,3},{3,2},{4,5},{5,4},{6,7},{7,6},{8,9},{9,8},{10,11... | collective-permute-start | bytes 7077896 | tf_op jit(solution)/shard_map/ppermute | solution.py:18
  802.3 30.9 %collective-permute-start.67 = (bf16[72,2048]{1,0:T(8,128)(2,1)S(1)}, bf16[72,2048]{1,0:T(8,128)(2,1)}, u32[]{:S(2)}, u32[]{:S(2)}) collective-permute-start(bf16[72,2048]{1,0:T(8,128)(2,1)S(1)} %pad_maximum_fusion.20), channel_id=1, source_target_pairs={{0,2},{1,3},{4,0},{5,1},{8,4},{9,5},{12,8},{13,9},{14,12},{15,13},... | collective-permute-start | bytes 884744 | tf_op jit(solution)/shard_map/ppermute | solution.py:33
  827.0 18.1 %collective-permute-start.74 = (bf16[128,2048]{1,0:T(8,128)(2,1)S(1)}, bf16[128,2048]{1,0:T(8,128)(2,1)S(1)}, u32[]{:S(2)}, u32[]{:S(2)}) collective-permute-start(bf16[128,2048]{1,0:T(8,128)(2,1)S(1)} %pad_maximum_fusion.15), channel_id=1, source_target_pairs={{0,4},{1,5},{4,8},{5,9},{8,12},{9,13},{12,14},{13,15},{14,10},{15,... | collective-permute-start | bytes 1572872 | tf_op jit(solution)/shard_map/ppermute | solution.py:33
  833.1 19.2 %collective-permute-start.78 = (bf16[128,2048]{1,0:T(8,128)(2,1)S(1)}, bf16[128,2048]{1,0:T(8,128)(2,1)S(1)}, u32[]{:S(2)}, u32[]{:S(2)}) collective-permute-start(bf16[128,2048]{1,0:T(8,128)(2,1)S(1)} %pad_maximum_fusion.16), channel_id=1, source_target_pairs={{0,2},{1,3},{4,0},{5,1},{8,4},{9,5},{12,8},{13,9},{14,12},{15,13},... | collective-permute-start | bytes 1572872 | tf_op jit(solution)/shard_map/ppermute | solution.py:33
  845.2 14.9 %collective-permute-start.75 = (bf16[128,2048]{1,0:T(8,128)(2,1)S(1)}, bf16[128,2048]{1,0:T(8,128)(2,1)S(1)}, u32[]{:S(2)}, u32[]{:S(2)}) collective-permute-start(bf16[128,2048]{1,0:T(8,128)(2,1)S(1)} %fusion.129), channel_id=1, source_target_pairs={{0,4},{1,5},{4,8},{5,9},{8,12},{9,13},{12,14},{13,15},{14,10},{15,... | collective-permute-start | bytes 1572872 | tf_op jit(solution)/shard_map/ppermute | solution.py:33
  852.3 19.0 %collective-permute-start.52 = (bf16[288,1152]{1,0:T(8,128)(2,1)S(1)}, bf16[288,1152]{1,0:T(8,128)(2,1)S(1)}, u32[]{:S(2)}, u32[]{:S(2)}) collective-permute-start(bf16[288,1152]{1,0:T(8,128)(2,1)S(1)} %pad_maximum_fusion.13), channel_id=1, source_target_pairs={{0,4},{1,5},{4,8},{5,9},{8,12},{9,13},{12,14},{13,15},{14,10},{15,... | collective-permute-start | bytes 1990664 | tf_op jit(solution)/shard_map/ppermute | solution.py:33
  852.4 24.8 %collective-permute-start.65 = (bf16[72,2048]{1,0:T(8,128)(2,1)S(1)}, bf16[72,2048]{1,0:T(8,128)(2,1)S(1)}, u32[]{:S(2)}, u32[]{:S(2)}) collective-permute-start(bf16[72,2048]{1,0:T(8,128)(2,1)S(1)} %get-tuple-element.46), channel_id=1, source_target_pairs={{0,4},{1,5},{4,8},{5,9},{8,12},{9,13},{12,14},{13,15},{14,10},{15,... | collective-permute-start | bytes 884744 | tf_op jit(solution)/shard_map/ppermute | solution.py:33
  860.1 18.2 %collective-permute-start.69 = (bf16[72,2048]{1,0:T(8,128)(2,1)S(1)}, bf16[72,2048]{1,0:T(8,128)(2,1)S(1)}, u32[]{:S(2)}, u32[]{:S(2)}) collective-permute-start(bf16[72,2048]{1,0:T(8,128)(2,1)S(1)} %fusion.148), channel_id=1, source_target_pairs={{0,2},{1,3},{4,0},{5,1},{8,4},{9,5},{12,8},{13,9},{14,12},{15,13},... | collective-permute-start | bytes 884744 | tf_op jit(solution)/shard_map/ppermute | solution.py:33
  877.2 18.8 %collective-permute-start.56 = (bf16[288,1152]{1,0:T(8,128)(2,1)S(1)}, bf16[288,1152]{1,0:T(8,128)(2,1)S(1)}, u32[]{:S(2)}, u32[]{:S(2)}) collective-permute-start(bf16[288,1152]{1,0:T(8,128)(2,1)S(1)} %pad_maximum_fusion.14), channel_id=1, source_target_pairs={{0,2},{1,3},{4,0},{5,1},{8,4},{9,5},{12,8},{13,9},{14,12},{15,13},... | collective-permute-start | bytes 1990664 | tf_op jit(solution)/shard_map/ppermute | solution.py:33
  878.3 20.2 %collective-permute-start.53 = (bf16[288,1152]{1,0:T(8,128)(2,1)S(1)}, bf16[288,1152]{1,0:T(8,128)(2,1)S(1)}, u32[]{:S(2)}, u32[]{:S(2)}) collective-permute-start(bf16[288,1152]{1,0:T(8,128)(2,1)S(1)} %fusion.103), channel_id=1, source_target_pairs={{0,4},{1,5},{4,8},{5,9},{8,12},{9,13},{12,14},{13,15},{14,10},{15,... | collective-permute-start | bytes 1990664 | tf_op jit(solution)/shard_map/ppermute | solution.py:33
  885.2 21.3 %collective-permute-start.76 = (bf16[128,2048]{1,0:T(8,128)(2,1)S(1)}, bf16[128,2048]{1,0:T(8,128)(2,1)S(1)}, u32[]{:S(2)}, u32[]{:S(2)}) collective-permute-start(bf16[128,2048]{1,0:T(8,128)(2,1)S(1)} %get-tuple-element.38), channel_id=1, source_target_pairs={{0,4},{1,5},{4,8},{5,9},{8,12},{9,13},{12,14},{13,15},{14,10},{15,... | collective-permute-start | bytes 1572872 | tf_op jit(solution)/shard_map/ppermute | solution.py:33
  903.2 17.8 %collective-permute-start.57 = (bf16[288,1152]{1,0:T(8,128)(2,1)S(1)}, bf16[288,1152]{1,0:T(8,128)(2,1)S(1)}, u32[]{:S(2)}, u32[]{:S(2)}) collective-permute-start(bf16[288,1152]{1,0:T(8,128)(2,1)S(1)} %get-tuple-element.31), channel_id=1, source_target_pairs={{0,2},{1,3},{4,0},{5,1},{8,4},{9,5},{12,8},{13,9},{14,12},{15,13},... | collective-permute-start | bytes 1990664 | tf_op jit(solution)/shard_map/ppermute | solution.py:33
  906.5 35.4 %collective-permute-start.38 = (bf16[576,512]{1,0:T(8,128)(2,1)S(1)}, bf16[576,512]{1,0:T(8,128)(2,1)}, u32[]{:S(2)}, u32[]{:S(2)}) collective-permute-start(bf16[576,512]{1,0:T(8,128)(2,1)S(1)} %bitcast.571), channel_id=1, source_target_pairs={{0,1},{1,0},{2,3},{3,2},{4,5},{5,4},{6,7},{7,6},{8,9},{9,8},{10,11... | collective-permute-start | bytes 1769480 | tf_op jit(solution)/shard_map/ppermute | solution.py:18
  910.6 89.0 %collective-permute-start.54 = (bf16[288,1152]{1,0:T(8,128)(2,1)}, bf16[288,1152]{1,0:T(8,128)(2,1)}, u32[]{:S(2)}, u32[]{:S(2)}) collective-permute-start(bf16[288,1152]{1,0:T(8,128)(2,1)} %get-tuple-element.30), channel_id=1, source_target_pairs={{0,4},{1,5},{4,8},{5,9},{8,12},{9,13},{12,14},{13,15},{14,10},{15,... | collective-permute-start | bytes 1990664 | tf_op jit(solution)/shard_map/ppermute | solution.py:33
  921.0 57.1 %collective-permute-start.81 = (bf16[128,2048]{1,0:T(8,128)(2,1)}, bf16[128,2048]{1,0:T(8,128)(2,1)}, u32[]{:S(2)}, u32[]{:S(2)}) collective-permute-start(bf16[128,2048]{1,0:T(8,128)(2,1)} %fusion.182), channel_id=1, source_target_pairs={{0,16},{16,0},{1,17},{17,1},{2,18},{18,2},{3,19},{19,3},{4,20},{20... | collective-permute-start | bytes 1572872 | tf_op jit(solution)/shard_map/ppermute | solution.py:22
  924.5 76.7 %collective-permute-start.58 = (bf16[288,1152]{1,0:T(8,128)(2,1)}, bf16[288,1152]{1,0:T(8,128)(2,1)}, u32[]{:S(2)}, u32[]{:S(2)}) collective-permute-start(bf16[288,1152]{1,0:T(8,128)(2,1)} %fusion.102), channel_id=1, source_target_pairs={{0,2},{1,3},{4,0},{5,1},{8,4},{9,5},{12,8},{13,9},{14,12},{15,13},... | collective-permute-start | bytes 1990664 | tf_op jit(solution)/shard_map/ppermute | solution.py:33
  969.2 52.5 %collective-permute-start.17 = (bf16[512,3456]{0,1:T(8,128)(2,1)}, bf16[512,3456]{0,1:T(8,128)(2,1)S(1)}, u32[]{:S(2)}, u32[]{:S(2)}) collective-permute-start(bf16[512,3456]{0,1:T(8,128)(2,1)} %bitcast.544), channel_id=1, source_target_pairs={{0,1},{1,0},{2,3},{3,2},{4,5},{5,4},{6,7},{7,6},{8,9},{9,8},{10,11... | collective-permute-start | bytes 10616840 | tf_op jit(solution)/shard_map/ppermute | solution.py:18
  977.4 44.2 %collective-permute-start.16 = (bf16[576,512]{1,0:T(8,128)(2,1)S(1)}, bf16[576,512]{1,0:T(8,128)(2,1)S(1)}, u32[]{:S(2)}, u32[]{:S(2)}) collective-permute-start(bf16[576,512]{1,0:T(8,128)(2,1)S(1)} %bitcast.576), channel_id=1, source_target_pairs={{0,1},{1,0},{2,3},{3,2},{4,5},{5,4},{6,7},{7,6},{8,9},{9,8},{10,11... | collective-permute-start | bytes 1769480 | tf_op jit(solution)/shard_map/ppermute | solution.py:18
  999.0 15.7 %collective-permute-start.41 = (bf16[72,4608]{1,0:T(8,128)(2,1)S(1)}, bf16[72,4608]{1,0:T(8,128)(2,1)S(1)}, u32[]{:S(2)}, u32[]{:S(2)}) collective-permute-start(bf16[72,4608]{1,0:T(8,128)(2,1)S(1)} %pad_maximum_fusion.11), channel_id=1, source_target_pairs={{0,4},{1,5},{4,8},{5,9},{8,12},{9,13},{12,14},{13,15},{14,10},{15,... | collective-permute-start | bytes 1990664 | tf_op jit(solution)/shard_map/ppermute | solution.py:33
  999.6 50.9 %collective-permute-start.45 = (bf16[72,4608]{1,0:T(8,128)(2,1)S(1)}, bf16[72,4608]{1,0:T(8,128)(2,1)}, u32[]{:S(2)}, u32[]{:S(2)}) collective-permute-start(bf16[72,4608]{1,0:T(8,128)(2,1)S(1)} %pad_maximum_fusion.12), channel_id=1, source_target_pairs={{0,2},{1,3},{4,0},{5,1},{8,4},{9,5},{12,8},{13,9},{14,12},{15,13},... | collective-permute-start | bytes 1990664 | tf_op jit(solution)/shard_map/ppermute | solution.py:33
  1003.1 15.4 %collective-permute-start.59 = (bf16[288,1152]{1,0:T(8,128)(2,1)S(1)}, bf16[288,1152]{1,0:T(8,128)(2,1)S(1)}, u32[]{:S(2)}, u32[]{:S(2)}) collective-permute-start(bf16[288,1152]{1,0:T(8,128)(2,1)S(1)} %fusion.169), channel_id=1, source_target_pairs={{0,16},{16,0},{1,17},{17,1},{2,18},{18,2},{3,19},{19,3},{4,20},{20... | collective-permute-start | bytes 1990664 | tf_op jit(solution)/shard_map/ppermute | solution.py:22
  1014.9 35.7 %collective-permute-start.42 = (bf16[72,4608]{1,0:T(8,128)(2,1)S(1)}, bf16[72,4608]{1,0:T(8,128)(2,1)}, u32[]{:S(2)}, u32[]{:S(2)}) collective-permute-start(bf16[72,4608]{1,0:T(8,128)(2,1)S(1)} %fusion.109), channel_id=1, source_target_pairs={{0,4},{1,5},{4,8},{5,9},{8,12},{9,13},{12,14},{13,15},{14,10},{15,... | collective-permute-start | bytes 1990664 | tf_op jit(solution)/shard_map/ppermute | solution.py:33
  1039.1 15.1 %collective-permute-start.23 = (bf16[72,3456]{1,0:T(8,128)(2,1)S(1)}, bf16[72,3456]{1,0:T(8,128)(2,1)S(1)}, u32[]{:S(2)}, u32[]{:S(2)}) collective-permute-start(bf16[72,3456]{1,0:T(8,128)(2,1)S(1)} %pad_maximum_fusion.18), channel_id=1, source_target_pairs={{0,2},{1,3},{4,0},{5,1},{8,4},{9,5},{12,8},{13,9},{14,12},{15,13},... | collective-permute-start | bytes 1493000 | tf_op jit(solution)/shard_map/ppermute | solution.py:33
  1050.0 14.3 %collective-permute-start.20 = (bf16[72,3456]{1,0:T(8,128)(2,1)S(1)}, bf16[72,3456]{1,0:T(8,128)(2,1)S(1)}, u32[]{:S(2)}, u32[]{:S(2)}) collective-permute-start(bf16[72,3456]{1,0:T(8,128)(2,1)S(1)} %fusion.135), channel_id=1, source_target_pairs={{0,4},{1,5},{4,8},{5,9},{8,12},{9,13},{12,14},{13,15},{14,10},{15,... | collective-permute-start | bytes 1493000 | tf_op jit(solution)/shard_map/ppermute | solution.py:33
  1052.1 17.3 %collective-permute-start.46 = (bf16[72,4608]{1,0:T(8,128)(2,1)S(1)}, bf16[72,4608]{1,0:T(8,128)(2,1)S(1)}, u32[]{:S(2)}, u32[]{:S(2)}) collective-permute-start(bf16[72,4608]{1,0:T(8,128)(2,1)S(1)} %get-tuple-element.37), channel_id=1, source_target_pairs={{0,2},{1,3},{4,0},{5,1},{8,4},{9,5},{12,8},{13,9},{14,12},{15,13},... | collective-permute-start | bytes 1990664 | tf_op jit(solution)/shard_map/ppermute | solution.py:33
  1053.7 28.6 %collective-permute-start.43 = (bf16[72,4608]{1,0:T(8,128)(2,1)S(1)}, bf16[72,4608]{1,0:T(8,128)(2,1)S(1)}, u32[]{:S(2)}, u32[]{:S(2)}) collective-permute-start(bf16[72,4608]{1,0:T(8,128)(2,1)S(1)} %get-tuple-element.36), channel_id=1, source_target_pairs={{0,4},{1,5},{4,8},{5,9},{8,12},{9,13},{12,14},{13,15},{14,10},{15,... | collective-permute-start | bytes 1990664 | tf_op jit(solution)/shard_map/ppermute | solution.py:33
  1064.6 15.5 %collective-permute-start.24 = (bf16[72,3456]{1,0:T(8,128)(2,1)S(1)}, bf16[72,3456]{1,0:T(8,128)(2,1)S(1)}, u32[]{:S(2)}, u32[]{:S(2)}) collective-permute-start(bf16[72,3456]{1,0:T(8,128)(2,1)S(1)} %get-tuple-element.45), channel_id=1, source_target_pairs={{0,2},{1,3},{4,0},{5,1},{8,4},{9,5},{12,8},{13,9},{14,12},{15,13},... | collective-permute-start | bytes 1493000 | tf_op jit(solution)/shard_map/ppermute | solution.py:33
  1069.6 23.5 %collective-permute-start.47 = (bf16[72,4608]{1,0:T(8,128)(2,1)S(1)}, bf16[72,4608]{1,0:T(8,128)(2,1)S(1)}, u32[]{:S(2)}, u32[]{:S(2)}) collective-permute-start(bf16[72,4608]{1,0:T(8,128)(2,1)S(1)} %fusion.108), channel_id=1, source_target_pairs={{0,2},{1,3},{4,0},{5,1},{8,4},{9,5},{12,8},{13,9},{14,12},{15,13},... | collective-permute-start | bytes 1990664 | tf_op jit(solution)/shard_map/ppermute | solution.py:33
  1071.6 23.6 %collective-permute-start.21 = (bf16[72,3456]{1,0:T(8,128)(2,1)S(1)}, bf16[72,3456]{1,0:T(8,128)(2,1)S(1)}, u32[]{:S(2)}, u32[]{:S(2)}) collective-permute-start(bf16[72,3456]{1,0:T(8,128)(2,1)S(1)} %get-tuple-element.44), channel_id=1, source_target_pairs={{0,4},{1,5},{4,8},{5,9},{8,12},{9,13},{12,14},{13,15},{14,10},{15,... | collective-permute-start | bytes 1493000 | tf_op jit(solution)/shard_map/ppermute | solution.py:33
  1080.2 18.2 %collective-permute-start.25 = (bf16[72,3456]{1,0:T(8,128)(2,1)S(1)}, bf16[72,3456]{1,0:T(8,128)(2,1)S(1)}, u32[]{:S(2)}, u32[]{:S(2)}) collective-permute-start(bf16[72,3456]{1,0:T(8,128)(2,1)S(1)} %fusion.134), channel_id=1, source_target_pairs={{0,2},{1,3},{4,0},{5,1},{8,4},{9,5},{12,8},{13,9},{14,12},{15,13},... | collective-permute-start | bytes 1493000 | tf_op jit(solution)/shard_map/ppermute | solution.py:33
  (141 other events, 2091.0 us)
Sparse Core Ops, SparseCore 0:
  10.2 75.5 all-gather.7
  87.9 41.6 all-gather.9
  131.9 87.3 all-gather.11
  221.5 86.8 all-gather.13
  310.5 51.5 all-gather.15
  364.1 73.4 all-gather.17
  439.9 43.4 all-gather.19
where the time goes:
time: 1130 us; the launch traced here: 1120 us
  waiting for transfers between devices  565 us (50%)
  matrix products  266 us (24%)
  local copies, waits for them, and re-layouts  92.7 us (8%)
  other arithmetic  92.5 us (8%)
  starting transfers between devices  88.8 us (8%)
  between operations  16.3 us (1%)
    ppermute x56, waiting for transfers between devices, hop(): return lax.ppermute(block, 'fsdp', pairs)  197 us
    all_gather x1, waiting for transfers between devices, shards(): lax.all_gather(w_fc2, 'fsdp', axis=0, tiled=True)  73.6 us
    dot_general x8, matrix products, product(): return jnp.dot(left, right, preferred_element_type=jnp.float32)  72 us
    all_gather x1, waiting for transfers between devices, shards(): lax.all_gather(w_proj2, 'fsdp', axis=0, tiled=True)  66.9 us
    dot_general x7, matrix products, input_grad(): jnp.einsum('ne,de->nd', grad, weight, preferred_element_type=jnp.float32)  59.2 us
    all_gather x1, waiting for transfers between devices, shards(): lax.all_gather(w_qkv, 'fsdp', axis=0, tiled=True)  58.8 us
    ppermute x56, starting transfers between devices, hop(): return lax.ppermute(block, 'fsdp', pairs)  57.3 us
    all_gather x1, waiting for transfers between devices, shards(): lax.all_gather(w_fc1, 'fsdp', axis=0, tiled=True)  51.1 us
  transfers between devices with their start and end apart: 100, of which 57 were waited for; matrix products, arithmetic and copies ran while one was open for 39% of the time, Pallas kernels for 0%

commit v1 on v0

--- a/solution.py
+++ b/solution.py
@@ -6,6 +6,24 @@
 
 HEADS = 16
 HIGH = lax.Precision.HIGHEST
+
+
+def gather_around(array, axis, dim):
+    ways, here, step = (lax.axis_size(axis), lax.axis_index(axis), array.shape[dim])
+    shape = [n * ways if d == dim else n for d, n in enumerate(array.shape)]
+    full = lax.dynamic_update_slice_in_dim(
+        jnp.zeros(shape, array.dtype), array, here * step, axis=dim
+    )
+    going_up = going_down = array
+    for far in range(1, ways // 2 + 1):
+        going_up = lax.ppermute(going_up, axis, [(d, (d + 1) % ways) for d in range(ways)])
+        full = lax.dynamic_update_slice_in_dim(full, going_up, (here - far) % ways * step, axis=dim)
+        if 2 * far < ways:
+            going_down = lax.ppermute(going_down, axis, [(d, (d - 1) % ways) for d in range(ways)])
+            full = lax.dynamic_update_slice_in_dim(
+                full, going_down, (here + far) % ways * step, axis=dim
+            )
+    return full
 
 
 def swapped(block, axis, apart):
@@ -179,7 +197,7 @@
     )
     head_set = (
         lax.all_gather(w_proj1, "fsdp", axis=0, tiled=True),
-        lax.all_gather(w_proj2, "fsdp", axis=0, tiled=True),
+        gather_around(w_proj2, "fsdp", 0),
         lax.all_gather(w_proj3, "fsdp", axis=0, tiled=True),
     )
     full_qkv, full_out, full_fc1, full_fc2 = block_set

time: 1130 us -> 1100 us (0.973)
  waiting for transfers between devices: 565 us -> 460 us
  starting transfers between devices: 88.8 us -> 130 us
  local copies, waits for them, and re-layouts: 92.7 us -> 122 us
    all_gather x1 -> x0, waiting for transfers between devices: 66.9 us -> none  [shards(): lax.all_gather(w_proj2, 'fsdp', axis=0, tiled=True)]
    all_gather x1, waiting for transfers between devices: 58.8 us -> 0.01 us  [shards(): lax.all_gather(w_qkv, 'fsdp', axis=0, tiled=True)]
    ppermute x0 -> x15, waiting for transfers between devices: none -> 44.4 us  [the longest x8 27.1 us: gather_around(): lax.ppermute(going_up, axis, [(d, (d + 1) % ways) for d in range(ways)])]
    ppermute x0 -> x15, starting transfers between devices: none -> 37.6 us  [the longest x7 20.1 us: gather_around(): lax.ppermute(going_down, axis, [(d, (d - 1) % ways) for d in range(ways)])]
    dynamic_update_slice x0 -> x16, local copies, waits for them, and re-layouts: none -> 20.8 us  [the longest x8 11 us: gather_around(): lax.dynamic_update_slice_in_dim(full, going_up, (here - far) % ways * ste...]
    all_gather x1, waiting for transfers between devices: 51.1 us -> 34.9 us  [shards(): lax.all_gather(w_fc1, 'fsdp', axis=0, tiled=True)]
    unnamed x182 -> x180, local copies, waits for them, and re-layouts: 31.1 us -> 36.4 us
  transfers between devices with their start and end apart: 100 -> 114, of which waited for: 57 -> 62; matrix products, arithmetic and copies ran while one was open for 39% -> 43% of each run, Pallas kernels for 0% -> 0%
where the time goes in v1:
time: 1100 us; the launch traced here: 1090 us
  waiting for transfers between devices  460 us (42%)
  matrix products  263 us (24%)
  starting transfers between devices  130 us (12%)
  local copies, waits for them, and re-layouts  122 us (11%)
  other arithmetic  94.1 us (9%)
  between operations  16.1 us (1%)
    ppermute x56, waiting for transfers between devices, hop(): return lax.ppermute(block, 'fsdp', pairs)  194 us
    all_gather x1, waiting for transfers between devices, shards(): lax.all_gather(w_fc2, 'fsdp', axis=0, tiled=True)  74.8 us
    dot_general x8, matrix products, product(): return jnp.dot(left, right, preferred_element_type=jnp.float32)  67.8 us
    dot_general x7, matrix products, input_grad(): jnp.einsum('ne,de->nd', grad, weight, preferred_element_type=jnp.float32)  61.3 us
    ppermute x56, starting transfers between devices, hop(): return lax.ppermute(block, 'fsdp', pairs)  56.5 us
    dot_general x7, matrix products, chip_grad(): total = jnp.dot(rows, grads, preferred_element_type=jnp.float32)  42.7 us
    all_gather x1, waiting for transfers between devices, shards(): lax.all_gather(w_proj1, 'fsdp', axis=0, tiled=True)  39.9 us
    unnamed x180, local copies, waits for them, and re-layouts  36.4 us
  transfers between devices with their start and end apart: 114, of which 62 were waited for; matrix products, arithmetic and copies ran while one was open for 43% of the time, Pallas kernels for 0%

profile of v1, /device:TPU:0, one launch (start us, length us, event | category | flops | bytes accessed | tf_op | source)
XLA Modules:
  0.0 1086.4 jit_solution(1570695205966443167)
XLA Ops:
  23.4 7.8 collective-permute-start.7
  36.8 9.4 collective-permute-done.7
  57.9 6.4 collective-permute-start.3
  72.1 6.2 collective-permute-done.10
  96.5 9.7 collective-permute-done.13
  106.2 10.0 convolution_convert_fusion
  138.2 7.6 collective-permute-done.16
  167.7 16.9 %fusion.244 = (f32[16,512]{1,0:T(8,128)S(1)}, f32[16,512,1024]{2,1,0:T(8,128)}) fusion(bf16[512,16,72]{0,2,1:T(8,128)(2,1)S(1)} %get-tuple-element.67, bf16[512,16,72]{0,2,1:T(8,128)(2,1)S(1)} %get-tuple-element.54, bf16[512,3,16,72]{0,3,2,1:T(8,128)(2,1)} %bitcast.488, pred[512,1024]{1,0:T(8,128)(4,1)S(1)} %broadcast_compare_fusion), kind=kOutput, calls=%fused_computation.468 | convolution fusion | flops 1237835776 | bytes 37650432 | tf_op jit(solution)/shard_map/qhd,khd->hqk/dot_general | solution.py:217
  184.6 14.4 %fusion = f32[16,512]{1,0:T(8,128)S(1)} fusion(f32[16,512,1024]{2,1,0:T(8,128)} %get-tuple-element.101, f32[16,512]{1,0:T(8,128)S(1)} %get-tuple-element.100), kind=kLoop, calls=%fused_computation.6 | loop fusion | flops 16769024 | bytes 33619968 | tf_op jit(solution)/shard_map/reduce_sum | solution.py:221
  199.6 15.8 %fusion.98 = bf16[16,72,512]{2,1,0:T(8,128)(2,1)S(1)} fusion(f32[16,512,1024]{2,1,0:T(8,128)} %get-tuple-element.101, f32[16,512]{1,0:T(8,128)S(1)} %fusion, f32[16,512]{1,0:T(8,128)S(1)} %get-tuple-element.100, bf16[512,16,72]{0,2,1:T(8,128)(2,1)} %get-tuple-element.66, bf16[512,16,72]{0,2,1:T(8,128)(2,1)} %get-tuple-element.52), kind=kOutput, calls=%fused_computation.150 | convolution fusion | flops 1238433792 | bytes 37158912 | tf_op jit(solution)/shard_map/hqk,khd->qhd/dot_general | solution.py:224
  222.5 34.9 %all-gather.11.cloned.1.call-done = bf16[1152,4608]{1,0:T(8,128)(2,1)} async-done(((bf16[72,4608]{1,0:T(8,128)(2,1)}), bf16[1152,4608]{1,0:T(8,128)(2,1)}) %all-gather.11.cloned.1.call-update) | async-done | bytes 10616848 | tf_op jit(solution)/shard_map/all_gather | solution.py:195
  257.4 14.2 %fusion.20 = (bf16[4608,512]{0,1:T(8,128)(2,1)}, f32[512,4608]{1,0:T(8,128)}) fusion(bf16[1152,4608]{1,0:T(8,128)(2,1)} %all-gather.11.cloned.1.call-done, f32[512,1152]{1,0:T(8,128)} %copy-done.5, f32[1152]{0:T(1024)S(1)} %get-tuple-element.91, f32[1152]{0:T(1024)S(1)} %get-tuple-element.92, f32[512]{0:T(512)S(1)} %fusion.216, ...), kind=kOutput, calls=%fused_computation.28 | convolution fusion | flops 5460000768 | bytes 27145216 | tf_op jit(solution)/shard_map/dot_general | solution.py:160
  271.6 74.8 %all-gather.13.cloned.1.call-done = bf16[4608,1152]{1,0:T(8,128)(2,1)} async-done(((bf16[288,1152]{1,0:T(8,128)(2,1)}), bf16[4608,1152]{1,0:T(8,128)(2,1)}) %all-gather.13.cloned.1.call-update) | async-done | bytes 10616848 | tf_op jit(solution)/shard_map/all_gather | solution.py:196
  346.4 13.9 %add_convert_fusion = (bf16[512,1152]{1,0:T(8,128)(2,1)S(1)}, f32[512,1152]{1,0:T(8,128)}) fusion(f32[512,1152]{1,0:T(8,128)} %copy-done.5, f32[1152]{0:T(1024)S(1)} %get-tuple-element.90, bf16[4608,1152]{1,0:T(8,128)(2,1)} %all-gather.13.cloned.1.call-done, f32[512,4608]{1,0:T(8,128)} %get-tuple-element.114), kind=kOutput, calls=%fused_computation.127 | convolution fusion | flops 5458821120 | bytes 25956864 | tf_op jit(solution)/shard_map/dot_general | solution.py:160
  360.3 39.9 %all-gather.15.cloned.1.call-done = bf16[1152,2048]{1,0:T(8,128)(2,1)} async-done(((bf16[72,2048]{1,0:T(8,128)(2,1)}), bf16[1152,2048]{1,0:T(8,128)(2,1)}) %all-gather.15.cloned.1.call-update) | async-done | bytes 4718608 | tf_op jit(solution)/shard_map/all_gather | solution.py:199
  400.1 7.1 fusion.54
  409.2 10.5 fusion.55
  419.7 26.3 %all-gather.17.cloned.1.call-done = bf16[2048,768]{1,0:T(8,128)(2,1)} async-done(((bf16[128,768]{1,0:T(8,128)(2,1)}), bf16[2048,768]{1,0:T(8,128)(2,1)}) %all-gather.17.cloned.1.call-update) | async-done | bytes 3145744 | tf_op jit(solution)/shard_map/all_gather | solution.py:201
  446.1 5.9 fusion.91
  458.0 11.3 %fusion.39 = bf16[512,2048]{1,0:T(8,128)(2,1)} fusion(f32[512,2048]{1,0:T(8,128)} %copy-done.81, bf16[512,2048]{1,0:T(8,128)(2,1)S(1)} %fusion.36, bf16[2048,2048]{1,0:T(8,128)(2,1)} %constant_dynamic-update-slice_fusion), kind=kOutput, calls=%fused_computation.53 | convolution fusion | flops 4305453056 | bytes 16777216 | tf_op jit(solution)/shard_map/ne,de->nd/dot_general | solution.py:164
  473.8 17.0 %fusion.12 = bf16[512,4608]{1,0:T(8,128)(2,1)} fusion(f32[512,4608]{1,0:T(8,128)} %get-tuple-element.114, bf16[512,1152]{1,0:T(8,128)(2,1)S(1)} %get-tuple-element.106, bf16[4608,1152]{1,0:T(8,128)(2,1)} %all-gather.13.cloned.1.call-done), kind=kOutput, calls=%fused_computation.20 | convolution fusion | flops 5483003904 | bytes 25952256 | tf_op jit(solution)/shard_map/ne,de->nd/dot_general | solution.py:164
  490.8 11.6 %multiply_reduce_fusion.2 = (f32[1152]{0:T(1024)S(1)}, f32[512]{0:T(512)S(1)}, f32[1152]{0:T(1024)S(1)}, f32[512,1152]{1,0:T(8,128)S(1)}) fusion(f32[512,1152]{1,0:T(8,128)S(1)} %copy-done.6, f32[512]{0:T(512)S(1)} %fusion.216, f32[512]{0:T(512)S(1)} %broadcast_multiply_fusion, f32[1152]{0:T(1024)S(1)} %get-tuple-element.92, ...), kind=kOutput, calls=%fused_computation.119 | convolution fusion | flops 5440534016 | bytes 20073984 | tf_op jit(solution)/shard_map/ne,de->nd/dot_general | solution.py:164
  514.1 15.7 %fusion.78 = f32[1024,16,72]{0,2,1:T(8,128)} fusion(bf16[512,16,72]{0,2,1:T(8,128)(2,1)S(1)} %bitcast.490, f32[16,512,1024]{2,1,0:T(8,128)} %get-tuple-element.101, f32[16,512]{1,0:T(8,128)S(1)} %copy-done.33), kind=kOutput, calls=%fused_computation.130 | convolution fusion | flops 1224736768 | bytes 39485440 | tf_op jit(solution)/shard_map/hqk,qhd->khd/dot_general | solution.py:280
  529.9 22.3 %multiply_reduce_fusion = (f32[16,512]{1,0:T(8,128)S(1)}, f32[16,512,1024]{2,1,0:T(8,128)}) fusion(f32[16,512,1024]{2,1,0:T(8,128)} %get-tuple-element.101, f32[16,512]{1,0:T(8,128)S(1)} %copy-done.33, bf16[512,16,72]{0,2,1:T(8,128)(2,1)S(1)} %bitcast.491, bf16[512,16,72]{0,2,1:T(8,128)(2,1)S(1)} %copy-done.20, bf16[512,16,72]{0,2,1:T(8,128)(2,1)S(1)} %copy-done.19), kind=kOutput, calls=%fused_computation.1 | convolution fusion | flops 1237835776 | bytes 70713344 | tf_op jit(solution)/shard_map/qhd,khd->hqk/dot_general | solution.py:271
  552.9 27.8 %multiply_convert_fusion = bf16[16,512,1024]{2,1,0:T(8,128)(2,1)} fusion(f32[16,512,1024]{2,1,0:T(8,128)} %get-tuple-element.110, f32[16,512,1024]{2,1,0:T(8,128)} %get-tuple-element.101, f32[16,512]{1,0:T(8,128)S(1)} %get-tuple-element.109, f32[16,512]{1,0:T(8,128)S(1)} %copy-done.33), kind=kLoop, calls=%fused_computation | loop fusion | flops 33554432 | bytes 83951616 | tf_op jit(solution)/shard_map/convert_element_type | solution.py:273
  580.7 11.3 %multiply_bitcast_fusion = f32[1024,16,72]{0,2,1:T(8,128)} fusion(bf16[16,512,1024]{2,1,0:T(8,128)(2,1)} %multiply_convert_fusion, bf16[512,3,16,72]{0,3,2,1:T(8,128)(2,1)} %bitcast.489), kind=kOutput, calls=%fused_computation.46 | convolution fusion | flops 1209139200 | bytes 22675456 | tf_op jit(solution)/shard_map/hqk,qhd->khd/dot_general | solution.py:278
  595.0 6.7 copy.33
  615.5 12.0 %constant_dynamic-slice_fusion.1 = (bf16[8,1,128,512]{2,1,0,3:T(2,128)(2,1)}, bf16[8,1,128,512]{2,1,0,3:T(2,128)(2,1)}, bf16[8,1,128,512]{2,1,0,3:T(2,128)(2,1)}, bf16[8,1,128,512]{2,1,0,3:T(2,128)(2,1)}) fusion(bf16[8,2,128,512]{2,1,0,3:T(2,128)(2,1)} %reshape.384, s32[]{:T(128)S(6)} %select_n.948, s32[]{:T(128)S(6)} %select_n.949, ...), kind=kLoop, calls=%fused_computation.374 | loop fusion | bytes 8388616 | tf_op jit(solution)/shard_map/jit(dynamic_index_in_dim)/dynamic_slice | solution.py:97
  627.5 6.2 copy.42
  652.9 6.0 copy.41
  658.9 9.0 fusion.100
  740.2 6.4 fusion.44
  768.9 8.6 fusion.29
  799.4 9.1 collective-permute-done.79
  819.5 6.5 collective-permute-done.90
  826.9 10.0 collective-permute-done.67
  853.1 8.9 collective-permute-done.71
  879.5 7.4 collective-permute-done.72
  895.3 8.9 fusion.66
  908.7 8.5 fusion.21
  954.3 8.2 collective-permute-done.55
  970.8 8.7 collective-permute-done.56
  989.2 7.2 fusion.25
  1006.2 9.2 collective-permute-done.34
  1020.0 9.8 collective-permute-done.35
  1037.7 8.4 collective-permute-done.39
  1047.8 11.1 %collective-permute-done.62 = bf16[72,4608]{1,0:T(8,128)(2,1)S(1)} collective-permute-done((bf16[72,4608]{1,0:T(8,128)(2,1)S(1)}, bf16[72,4608]{1,0:T(8,128)(2,1)S(1)}, u32[]{:S(2)}, u32[]{:S(2)}) %collective-permute-start.62) | collective-permute-done | bytes 663584 | tf_op jit(solution)/shard_map/ppermute | solution.py:51
  1066.3 6.4 collective-permute-done.63
  (577 shorter events, 438.4 us)
Async XLA Ops:
  7.2 98.9 %all-gather.7.cloned.1.call-start = ((), (), s32[]{:S(2)}) async-start(), calls=%async_computation | async-start | bytes 8460288 | tf_op jit(solution)/shard_map/all_gather | solution.py:193
  7.9 207.5 %all-gather.9.cloned.1.call-start = ((), (), s32[]{:S(2)}) async-start(), calls=%async_computation.1 | async-start | bytes 2820096 | tf_op jit(solution)/shard_map/all_gather | solution.py:194
  8.7 248.7 %all-gather.11.cloned.1.call-start = ((), (), s32[]{:S(2)}) async-start(), calls=%async_computation.2 | async-start | bytes 11280384 | tf_op jit(solution)/shard_map/all_gather | solution.py:195
  9.4 337.0 %all-gather.13.cloned.1.call-start = ((), (), s32[]{:S(2)}) async-start(), calls=%async_computation.3 | async-start | bytes 11280384 | tf_op jit(solution)/shard_map/all_gather | solution.py:196
  10.0 390.1 %all-gather.15.cloned.1.call-start = ((), (), s32[]{:S(2)}) async-start(), calls=%async_computation.4 | async-start | bytes 5013504 | tf_op jit(solution)/shard_map/all_gather | solution.py:199
  10.6 435.5 %all-gather.17.cloned.1.call-start = ((), (), s32[]{:S(2)}) async-start(), calls=%async_computation.5 | async-start | bytes 3342336 | tf_op jit(solution)/shard_map/all_gather | solution.py:201
  11.1 25.6 %collective-permute-start.6 = (bf16[128,2048]{1,0:T(8,128)(2,1)}, bf16[128,2048]{1,0:T(8,128)(2,1)}, u32[]{:S(2)}, u32[]{:S(2)}) collective-permute-start(bf16[128,2048]{1,0:T(8,128)(2,1)} %param.24), channel_id=1, source_target_pairs={{0,15},{1,0},{2,1},{3,2},{4,3},{5,4},{6,5},{7,6},{8,7},{9,8},{10,9... | collective-permute-start | bytes 1572872 | tf_op jit(solution)/shard_map/ppermute | solution.py:22
  18.6 27.7 %collective-permute-start = (f32[432]{0:T(512)S(1)}, f32[432]{0:T(512)S(1)}, u32[]{:S(2)}, u32[]{:S(2)}) collective-permute-start(f32[432]{0:T(512)S(1)} %bitcast.580), channel_id=1, source_target_pairs={{0,1},{1,0},{2,3},{3,2},{4,5},{5,4},{6,7},{7,6},{8,9},{9,8},{10,11... | collective-permute-start | bytes 5192 | tf_op jit(solution)/shard_map/ppermute | solution.py:36
  18.6 45.7 %collective-permute-start.29 = (f32[1,1152]{1,0:T(1,128)S(1)}, f32[1,1152]{1,0:T(1,128)S(1)}, u32[]{:S(2)}, u32[]{:S(2)}) collective-permute-start(f32[1,1152]{1,0:T(1,128)S(1)} %get-tuple-element.22), channel_id=1, source_target_pairs={{0,16},{16,0},{1,17},{17,1},{2,18},{18,2},{3,19},{19,3},{4,20},{20... | collective-permute-start | bytes 13832 | tf_op jit(solution)/shard_map/ppermute | solution.py:40
  23.4 22.8 %collective-permute-start.7 = (bf16[128,2048]{1,0:T(8,128)(2,1)}, bf16[128,2048]{1,0:T(8,128)(2,1)}, u32[]{:S(2)}, u32[]{:S(2)}) collective-permute-start(bf16[128,2048]{1,0:T(8,128)(2,1)} %collective-permute-done.5), channel_id=1, source_target_pairs={{0,1},{1,2},{2,3},{3,4},{4,5},{5,6},{6,7},{7,8},{8,9},{9,10},{10,1... | collective-permute-start | bytes 1572872 | tf_op jit(solution)/shard_map/ppermute | solution.py:19
  36.8 30.9 %collective-permute-start.8 = (bf16[128,2048]{1,0:T(8,128)(2,1)}, bf16[128,2048]{1,0:T(8,128)(2,1)S(1)}, u32[]{:S(2)}, u32[]{:S(2)}) collective-permute-start(bf16[128,2048]{1,0:T(8,128)(2,1)} %collective-permute-done.6), channel_id=1, source_target_pairs={{0,15},{1,0},{2,1},{3,2},{4,3},{5,4},{6,5},{7,6},{8,7},{9,8},{10,9... | collective-permute-start | bytes 1572872 | tf_op jit(solution)/shard_map/ppermute | solution.py:22
  46.2 21.5 %collective-permute-start.9 = (bf16[128,2048]{1,0:T(8,128)(2,1)}, bf16[128,2048]{1,0:T(8,128)(2,1)}, u32[]{:S(2)}, u32[]{:S(2)}) collective-permute-start(bf16[128,2048]{1,0:T(8,128)(2,1)} %collective-permute-done.7), channel_id=1, source_target_pairs={{0,1},{1,2},{2,3},{3,4},{4,5},{5,6},{6,7},{7,8},{8,9},{9,10},{10,1... | collective-permute-start | bytes 1572872 | tf_op jit(solution)/shard_map/ppermute | solution.py:19
  67.8 18.1 %collective-permute-start.11 = (bf16[128,2048]{1,0:T(8,128)(2,1)}, bf16[128,2048]{1,0:T(8,128)(2,1)S(1)}, u32[]{:S(2)}, u32[]{:S(2)}) collective-permute-start(bf16[128,2048]{1,0:T(8,128)(2,1)} %collective-permute-done.9), channel_id=1, source_target_pairs={{0,1},{1,2},{2,3},{3,4},{4,5},{5,6},{6,7},{7,8},{8,9},{9,10},{10,1... | collective-permute-start | bytes 1572872 | tf_op jit(solution)/shard_map/ppermute | solution.py:19
  85.8 20.3 %collective-permute-start.13 = (bf16[128,2048]{1,0:T(8,128)(2,1)S(1)}, bf16[128,2048]{1,0:T(8,128)(2,1)}, u32[]{:S(2)}, u32[]{:S(2)}) collective-permute-start(bf16[128,2048]{1,0:T(8,128)(2,1)S(1)} %collective-permute-done.11), channel_id=1, source_target_pairs={{0,1},{1,2},{2,3},{3,4},{4,5},{5,6},{6,7},{7,8},{8,9},{9,10},{10,1... | collective-permute-start | bytes 1572872 | tf_op jit(solution)/shard_map/ppermute | solution.py:19
  95.2 32.9 %collective-permute-start.14 = (bf16[128,2048]{1,0:T(8,128)(2,1)}, bf16[128,2048]{1,0:T(8,128)(2,1)}, u32[]{:S(2)}, u32[]{:S(2)}) collective-permute-start(bf16[128,2048]{1,0:T(8,128)(2,1)} %collective-permute-done.12), channel_id=1, source_target_pairs={{0,15},{1,0},{2,1},{3,2},{4,3},{5,4},{6,5},{7,6},{8,7},{9,8},{10,9... | collective-permute-start | bytes 1572872 | tf_op jit(solution)/shard_map/ppermute | solution.py:22
  106.1 28.3 %collective-permute-start.15 = (bf16[128,2048]{1,0:T(8,128)(2,1)}, bf16[128,2048]{1,0:T(8,128)(2,1)S(1)}, u32[]{:S(2)}, u32[]{:S(2)}) collective-permute-start(bf16[128,2048]{1,0:T(8,128)(2,1)} %collective-permute-done.13), channel_id=1, source_target_pairs={{0,1},{1,2},{2,3},{3,4},{4,5},{5,6},{6,7},{7,8},{8,9},{9,10},{10,1... | collective-permute-start | bytes 1572872 | tf_op jit(solution)/shard_map/ppermute | solution.py:19
  125.2 41.2 %collective-permute-start.4 = (bf16[2,512,16,72]{1,3,2,0:T(8,128)(2,1)S(1)}, bf16[2,512,16,72]{1,3,2,0:T(8,128)(2,1)S(1)}, u32[]{:S(2)}, u32[]{:S(2)}) collective-permute-start(bf16[2,512,16,72]{1,3,2,0:T(8,128)(2,1)S(1)} %pad_maximum_fusion.2), channel_id=1, source_target_pairs={{0,1},{1,0},{2,3},{3,2},{4,5},{5,4},{6,7},{7,6},{8,9},{9,8},{10,11... | collective-permute-start | bytes 7077896 | tf_op jit(solution)/shard_map/ppermute | solution.py:36
  222.4 456.0 %collective-permute-start.42 = (bf16[576,512]{1,0:T(8,128)(2,1)}, bf16[576,512]{1,0:T(8,128)(2,1)}, u32[]{:S(2)}, u32[]{:S(2)}) collective-permute-start(bf16[576,512]{1,0:T(8,128)(2,1)} %bitcast.49), channel_id=1, source_target_pairs={{0,1},{1,0},{2,3},{3,2},{4,5},{5,4},{6,7},{7,6},{8,9},{9,8},{10,11... | collective-permute-start | bytes 1769480 | tf_op jit(solution)/shard_map/ppermute | solution.py:36
  552.2 127.1 %collective-permute-start.43 = (bf16[512,1152]{1,0:T(8,128)(2,1)}, bf16[512,1152]{1,0:T(8,128)(2,1)}, u32[]{:S(2)}, u32[]{:S(2)}) collective-permute-start(bf16[512,1152]{1,0:T(8,128)(2,1)} %multiply_convert_fusion.6), channel_id=1, source_target_pairs={{0,1},{1,0},{2,3},{3,2},{4,5},{5,4},{6,7},{7,6},{8,9},{9,8},{10,11... | collective-permute-start | bytes 3538952 | tf_op jit(solution)/shard_map/ppermute | solution.py:36
  552.4 178.3 %collective-permute-start.76 = (bf16[512,2048]{1,0:T(8,128)(2,1)}, bf16[512,2048]{1,0:T(8,128)(2,1)}, u32[]{:S(2)}, u32[]{:S(2)}) collective-permute-start(bf16[512,2048]{1,0:T(8,128)(2,1)} %fusion.39), channel_id=1, source_target_pairs={{0,1},{1,0},{2,3},{3,2},{4,5},{5,4},{6,7},{7,6},{8,9},{9,8},{10,11... | collective-permute-start | bytes 6291464 | tf_op jit(solution)/shard_map/ppermute | solution.py:36
  552.7 115.3 %collective-permute-start.98 = (bf16[512,768]{1,0:T(8,128)(2,1)}, bf16[512,768]{1,0:T(8,128)(2,1)}, u32[]{:S(2)}, u32[]{:S(2)}) collective-permute-start(bf16[512,768]{1,0:T(8,128)(2,1)} %fusion.94), channel_id=1, source_target_pairs={{0,1},{1,0},{2,3},{3,2},{4,5},{5,4},{6,7},{7,6},{8,9},{9,8},{10,11... | collective-permute-start | bytes 2359304 | tf_op jit(solution)/shard_map/ppermute | solution.py:36
  633.7 34.2 %collective-permute-start.97 = (bf16[1024,512]{1,0:T(8,128)(2,1)}, bf16[1024,512]{1,0:T(8,128)(2,1)}, u32[]{:S(2)}, u32[]{:S(2)}) collective-permute-start(bf16[1024,512]{1,0:T(8,128)(2,1)} %bitcast.127), channel_id=1, source_target_pairs={{0,1},{1,0},{2,3},{3,2},{4,5},{5,4},{6,7},{7,6},{8,9},{9,8},{10,11... | collective-permute-start | bytes 3145736 | tf_op jit(solution)/shard_map/ppermute | solution.py:36
  676.7 62.0 %collective-permute-start.87 = (bf16[512,2048]{1,0:T(8,128)(2,1)S(1)}, bf16[512,2048]{1,0:T(8,128)(2,1)S(1)}, u32[]{:S(2)}, u32[]{:S(2)}) collective-permute-start(bf16[512,2048]{1,0:T(8,128)(2,1)S(1)} %copy-done.73), channel_id=1, source_target_pairs={{0,1},{1,0},{2,3},{3,2},{4,5},{5,4},{6,7},{7,6},{8,9},{9,8},{10,11... | collective-permute-start | bytes 6291464 | tf_op jit(solution)/shard_map/ppermute | solution.py:36
  678.3 51.9 %collective-permute-start.75 = (bf16[576,512]{1,0:T(8,128)(2,1)S(1)}, bf16[576,512]{1,0:T(8,128)(2,1)S(1)}, u32[]{:S(2)}, u32[]{:S(2)}) collective-permute-start(bf16[576,512]{1,0:T(8,128)(2,1)S(1)} %bitcast.573), channel_id=1, source_target_pairs={{0,1},{1,0},{2,3},{3,2},{4,5},{5,4},{6,7},{7,6},{8,9},{9,8},{10,11... | collective-permute-start | bytes 1769480 | tf_op jit(solution)/shard_map/ppermute | solution.py:36
  726.1 182.7 %collective-permute-start.54 = (bf16[512,4608]{1,0:T(8,128)(2,1)}, bf16[512,4608]{1,0:T(8,128)(2,1)}, u32[]{:S(2)}, u32[]{:S(2)}) collective-permute-start(bf16[512,4608]{1,0:T(8,128)(2,1)} %fusion.12), channel_id=1, source_target_pairs={{0,1},{1,0},{2,3},{3,2},{4,5},{5,4},{6,7},{7,6},{8,9},{9,8},{10,11... | collective-permute-start | bytes 14155784 | tf_op jit(solution)/shard_map/ppermute | solution.py:36
  730.1 36.9 %collective-permute-start.65 = (bf16[512,1152]{1,0:T(8,128)(2,1)S(1)}, bf16[512,1152]{1,0:T(8,128)(2,1)}, u32[]{:S(2)}, u32[]{:S(2)}) collective-permute-start(bf16[512,1152]{1,0:T(8,128)(2,1)S(1)} %copy-done.77), channel_id=1, source_target_pairs={{0,1},{1,0},{2,3},{3,2},{4,5},{5,4},{6,7},{7,6},{8,9},{9,8},{10,11... | collective-permute-start | bytes 3538952 | tf_op jit(solution)/shard_map/ppermute | solution.py:36
  730.2 160.3 %collective-permute-start.20 = (f32[2,512,16,72]{1,3,2,0:T(8,128)}, f32[2,512,16,72]{1,3,2,0:T(8,128)}, u32[]{:S(2)}, u32[]{:S(2)}) collective-permute-start(f32[2,512,16,72]{1,3,2,0:T(8,128)} %pad_maximum_fusion), channel_id=1, source_target_pairs={{0,1},{1,0},{2,3},{3,2},{4,5},{5,4},{6,7},{7,6},{8,9},{9,8},{10,11... | collective-permute-start | bytes 14155784 | tf_op jit(solution)/shard_map/ppermute | solution.py:36
  738.6 29.7 %collective-permute-start.64 = (bf16[2304,512]{1,0:T(8,128)(2,1)S(1)}, bf16[2304,512]{1,0:T(8,128)(2,1)}, u32[]{:S(2)}, u32[]{:S(2)}) collective-permute-start(bf16[2304,512]{1,0:T(8,128)(2,1)S(1)} %bitcast.565), channel_id=1, source_target_pairs={{0,1},{1,0},{2,3},{3,2},{4,5},{5,4},{6,7},{7,6},{8,9},{9,8},{10,11... | collective-permute-start | bytes 7077896 | tf_op jit(solution)/shard_map/ppermute | solution.py:36
  768.2 30.6 %collective-permute-start.82 = (bf16[72,2048]{1,0:T(8,128)(2,1)}, bf16[72,2048]{1,0:T(8,128)(2,1)}, u32[]{:S(2)}, u32[]{:S(2)}) collective-permute-start(bf16[72,2048]{1,0:T(8,128)(2,1)} %pad_maximum_fusion.20), channel_id=1, source_target_pairs={{0,2},{1,3},{4,0},{5,1},{8,4},{9,5},{12,8},{13,9},{14,12},{15,13},... | collective-permute-start | bytes 884744 | tf_op jit(solution)/shard_map/ppermute | solution.py:51
  791.8 19.1 %collective-permute-start.89 = (bf16[128,2048]{1,0:T(8,128)(2,1)S(1)}, bf16[128,2048]{1,0:T(8,128)(2,1)S(1)}, u32[]{:S(2)}, u32[]{:S(2)}) collective-permute-start(bf16[128,2048]{1,0:T(8,128)(2,1)S(1)} %pad_maximum_fusion.15), channel_id=1, source_target_pairs={{0,4},{1,5},{4,8},{5,9},{8,12},{9,13},{12,14},{13,15},{14,10},{15,... | collective-permute-start | bytes 1572872 | tf_op jit(solution)/shard_map/ppermute | solution.py:51
  798.9 20.6 %collective-permute-start.93 = (bf16[128,2048]{1,0:T(8,128)(2,1)S(1)}, bf16[128,2048]{1,0:T(8,128)(2,1)S(1)}, u32[]{:S(2)}, u32[]{:S(2)}) collective-permute-start(bf16[128,2048]{1,0:T(8,128)(2,1)S(1)} %pad_maximum_fusion.16), channel_id=1, source_target_pairs={{0,2},{1,3},{4,0},{5,1},{8,4},{9,5},{12,8},{13,9},{14,12},{15,13},... | collective-permute-start | bytes 1572872 | tf_op jit(solution)/shard_map/ppermute | solution.py:51
  816.6 20.3 %collective-permute-start.67 = (bf16[288,1152]{1,0:T(8,128)(2,1)S(1)}, bf16[288,1152]{1,0:T(8,128)(2,1)S(1)}, u32[]{:S(2)}, u32[]{:S(2)}) collective-permute-start(bf16[288,1152]{1,0:T(8,128)(2,1)S(1)} %pad_maximum_fusion.13), channel_id=1, source_target_pairs={{0,4},{1,5},{4,8},{5,9},{8,12},{9,13},{12,14},{13,15},{14,10},{15,... | collective-permute-start | bytes 1990664 | tf_op jit(solution)/shard_map/ppermute | solution.py:51
  819.4 23.8 %collective-permute-start.80 = (bf16[72,2048]{1,0:T(8,128)(2,1)S(1)}, bf16[72,2048]{1,0:T(8,128)(2,1)S(1)}, u32[]{:S(2)}, u32[]{:S(2)}) collective-permute-start(bf16[72,2048]{1,0:T(8,128)(2,1)S(1)} %get-tuple-element.46), channel_id=1, source_target_pairs={{0,4},{1,5},{4,8},{5,9},{8,12},{9,13},{12,14},{13,15},{14,10},{15,... | collective-permute-start | bytes 884744 | tf_op jit(solution)/shard_map/ppermute | solution.py:51
  826.0 18.2 %collective-permute-start.84 = (bf16[72,2048]{1,0:T(8,128)(2,1)S(1)}, bf16[72,2048]{1,0:T(8,128)(2,1)S(1)}, u32[]{:S(2)}, u32[]{:S(2)}) collective-permute-start(bf16[72,2048]{1,0:T(8,128)(2,1)S(1)} %fusion.148), channel_id=1, source_target_pairs={{0,2},{1,3},{4,0},{5,1},{8,4},{9,5},{12,8},{13,9},{14,12},{15,13},... | collective-permute-start | bytes 884744 | tf_op jit(solution)/shard_map/ppermute | solution.py:51
  843.3 18.8 %collective-permute-start.71 = (bf16[288,1152]{1,0:T(8,128)(2,1)S(1)}, bf16[288,1152]{1,0:T(8,128)(2,1)S(1)}, u32[]{:S(2)}, u32[]{:S(2)}) collective-permute-start(bf16[288,1152]{1,0:T(8,128)(2,1)S(1)} %pad_maximum_fusion.14), channel_id=1, source_target_pairs={{0,2},{1,3},{4,0},{5,1},{8,4},{9,5},{12,8},{13,9},{14,12},{15,13},... | collective-permute-start | bytes 1990664 | tf_op jit(solution)/shard_map/ppermute | solution.py:51
  844.1 20.3 %collective-permute-start.68 = (bf16[288,1152]{1,0:T(8,128)(2,1)S(1)}, bf16[288,1152]{1,0:T(8,128)(2,1)S(1)}, u32[]{:S(2)}, u32[]{:S(2)}) collective-permute-start(bf16[288,1152]{1,0:T(8,128)(2,1)S(1)} %fusion.103), channel_id=1, source_target_pairs={{0,4},{1,5},{4,8},{5,9},{8,12},{9,13},{12,14},{13,15},{14,10},{15,... | collective-permute-start | bytes 1990664 | tf_op jit(solution)/shard_map/ppermute | solution.py:51
  851.0 19.9 %collective-permute-start.91 = (bf16[128,2048]{1,0:T(8,128)(2,1)S(1)}, bf16[128,2048]{1,0:T(8,128)(2,1)S(1)}, u32[]{:S(2)}, u32[]{:S(2)}) collective-permute-start(bf16[128,2048]{1,0:T(8,128)(2,1)S(1)} %get-tuple-element.38), channel_id=1, source_target_pairs={{0,4},{1,5},{4,8},{5,9},{8,12},{9,13},{12,14},{13,15},{14,10},{15,... | collective-permute-start | bytes 1572872 | tf_op jit(solution)/shard_map/ppermute | solution.py:51
  871.0 36.0 %collective-permute-start.53 = (bf16[576,512]{1,0:T(8,128)(2,1)S(1)}, bf16[576,512]{1,0:T(8,128)(2,1)}, u32[]{:S(2)}, u32[]{:S(2)}) collective-permute-start(bf16[576,512]{1,0:T(8,128)(2,1)S(1)} %bitcast.571), channel_id=1, source_target_pairs={{0,1},{1,0},{2,3},{3,2},{4,5},{5,4},{6,7},{7,6},{8,9},{9,8},{10,11... | collective-permute-start | bytes 1769480 | tf_op jit(solution)/shard_map/ppermute | solution.py:36
  876.5 89.1 %collective-permute-start.69 = (bf16[288,1152]{1,0:T(8,128)(2,1)}, bf16[288,1152]{1,0:T(8,128)(2,1)}, u32[]{:S(2)}, u32[]{:S(2)}) collective-permute-start(bf16[288,1152]{1,0:T(8,128)(2,1)} %get-tuple-element.30), channel_id=1, source_target_pairs={{0,4},{1,5},{4,8},{5,9},{8,12},{9,13},{12,14},{13,15},{14,10},{15,... | collective-permute-start | bytes 1990664 | tf_op jit(solution)/shard_map/ppermute | solution.py:51
  886.8 56.0 %collective-permute-start.96 = (bf16[128,2048]{1,0:T(8,128)(2,1)}, bf16[128,2048]{1,0:T(8,128)(2,1)}, u32[]{:S(2)}, u32[]{:S(2)}) collective-permute-start(bf16[128,2048]{1,0:T(8,128)(2,1)} %fusion.182), channel_id=1, source_target_pairs={{0,16},{16,0},{1,17},{17,1},{2,18},{18,2},{3,19},{19,3},{4,20},{20... | collective-permute-start | bytes 1572872 | tf_op jit(solution)/shard_map/ppermute | solution.py:40
  890.5 76.3 %collective-permute-start.73 = (bf16[288,1152]{1,0:T(8,128)(2,1)}, bf16[288,1152]{1,0:T(8,128)(2,1)}, u32[]{:S(2)}, u32[]{:S(2)}) collective-permute-start(bf16[288,1152]{1,0:T(8,128)(2,1)} %fusion.102), channel_id=1, source_target_pairs={{0,2},{1,3},{4,0},{5,1},{8,4},{9,5},{12,8},{13,9},{14,12},{15,13},... | collective-permute-start | bytes 1990664 | tf_op jit(solution)/shard_map/ppermute | solution.py:51
  934.0 53.2 %collective-permute-start.32 = (bf16[512,3456]{0,1:T(8,128)(2,1)}, bf16[512,3456]{0,1:T(8,128)(2,1)S(1)}, u32[]{:S(2)}, u32[]{:S(2)}) collective-permute-start(bf16[512,3456]{0,1:T(8,128)(2,1)} %bitcast.544), channel_id=1, source_target_pairs={{0,1},{1,0},{2,3},{3,2},{4,5},{5,4},{6,7},{7,6},{8,9},{9,8},{10,11... | collective-permute-start | bytes 10616840 | tf_op jit(solution)/shard_map/ppermute | solution.py:36
  942.2 45.0 %collective-permute-start.31 = (bf16[576,512]{1,0:T(8,128)(2,1)S(1)}, bf16[576,512]{1,0:T(8,128)(2,1)S(1)}, u32[]{:S(2)}, u32[]{:S(2)}) collective-permute-start(bf16[576,512]{1,0:T(8,128)(2,1)S(1)} %bitcast.576), channel_id=1, source_target_pairs={{0,1},{1,0},{2,3},{3,2},{4,5},{5,4},{6,7},{7,6},{8,9},{9,8},{10,11... | collective-permute-start | bytes 1769480 | tf_op jit(solution)/shard_map/ppermute | solution.py:36
  965.6 50.8 %collective-permute-start.60 = (bf16[72,4608]{1,0:T(8,128)(2,1)}, bf16[72,4608]{1,0:T(8,128)(2,1)}, u32[]{:S(2)}, u32[]{:S(2)}) collective-permute-start(bf16[72,4608]{1,0:T(8,128)(2,1)} %pad_maximum_fusion.12), channel_id=1, source_target_pairs={{0,2},{1,3},{4,0},{5,1},{8,4},{9,5},{12,8},{13,9},{14,12},{15,13},... | collective-permute-start | bytes 1990664 | tf_op jit(solution)/shard_map/ppermute | solution.py:51
  980.5 35.9 %collective-permute-start.57 = (bf16[72,4608]{1,0:T(8,128)(2,1)}, bf16[72,4608]{1,0:T(8,128)(2,1)}, u32[]{:S(2)}, u32[]{:S(2)}) collective-permute-start(bf16[72,4608]{1,0:T(8,128)(2,1)} %fusion.109), channel_id=1, source_target_pairs={{0,4},{1,5},{4,8},{5,9},{8,12},{9,13},{12,14},{13,15},{14,10},{15,... | collective-permute-start | bytes 1990664 | tf_op jit(solution)/shard_map/ppermute | solution.py:51
  1019.2 28.6 %collective-permute-start.58 = (bf16[72,4608]{1,0:T(8,128)(2,1)S(1)}, bf16[72,4608]{1,0:T(8,128)(2,1)S(1)}, u32[]{:S(2)}, u32[]{:S(2)}) collective-permute-start(bf16[72,4608]{1,0:T(8,128)(2,1)S(1)} %get-tuple-element.36), channel_id=1, source_target_pairs={{0,4},{1,5},{4,8},{5,9},{8,12},{9,13},{12,14},{13,15},{14,10},{15,... | collective-permute-start | bytes 1990664 | tf_op jit(solution)/shard_map/ppermute | solution.py:51
  1035.6 23.3 %collective-permute-start.62 = (bf16[72,4608]{1,0:T(8,128)(2,1)S(1)}, bf16[72,4608]{1,0:T(8,128)(2,1)S(1)}, u32[]{:S(2)}, u32[]{:S(2)}) collective-permute-start(bf16[72,4608]{1,0:T(8,128)(2,1)S(1)} %fusion.108), channel_id=1, source_target_pairs={{0,2},{1,3},{4,0},{5,1},{8,4},{9,5},{12,8},{13,9},{14,12},{15,13},... | collective-permute-start | bytes 1990664 | tf_op jit(solution)/shard_map/ppermute | solution.py:51
  1037.1 23.9 %collective-permute-start.36 = (bf16[72,3456]{1,0:T(8,128)(2,1)S(1)}, bf16[72,3456]{1,0:T(8,128)(2,1)S(1)}, u32[]{:S(2)}, u32[]{:S(2)}) collective-permute-start(bf16[72,3456]{1,0:T(8,128)(2,1)S(1)} %get-tuple-element.44), channel_id=1, source_target_pairs={{0,4},{1,5},{4,8},{5,9},{8,12},{9,13},{12,14},{13,15},{14,10},{15,... | collective-permute-start | bytes 1493000 | tf_op jit(solution)/shard_map/ppermute | solution.py:51
  (154 other events, 2265.9 us)
Sparse Core Ops, SparseCore 0:
  10.2 94.8 all-gather.6
  107.3 55.5 all-gather.8
  165.1 92.2 all-gather.10
  259.5 86.8 all-gather.12
  348.6 51.5 all-gather.14
  402.3 43.7 all-gather.16
